TPU v7x, 32 devices: a whole 2x2x4 slice. The times are simulated.
32 devices in a mesh: dp: 16 (over z, y, core), tensor: 2 (over x).
Axes of the slice: x: 2, y: 2, z: 4, core: 2. Of those that a mesh axis runs over, the one named last changes fastest.
Arguments:
- tokens: bfloat16 [32, 448, 1024], P('dp'), may hold values from -6 to 6
- encoded: bfloat16 [32, 1500, 1024], P('dp'), may hold values from -6 to 6
- cotangent: bfloat16 [32, 448, 1024], P('dp'), may hold values from -6 to 6
- self_gain: bfloat16 [1024], replicated, may hold values from 0.5 to 1.5
- self_shift: bfloat16 [1024], replicated, may hold values from -1.75 to 1.75
- self_query: bfloat16 [1024, 1024], P(None, 'tensor'), may hold values from -0.25 to 0.25
- self_query_bias: bfloat16 [1024], P('tensor'), may hold values from -1.75 to 1.75
- self_key: bfloat16 [1024, 1024], P(None, 'tensor'), may hold values from -0.1875 to 0.1875
- self_value: bfloat16 [1024, 1024], P(None, 'tensor'), may hold values from -0.1875 to 0.1875
- self_value_bias: bfloat16 [1024], P('tensor'), may hold values from -1.75 to 1.75
- self_mixer: bfloat16 [1024, 1024], P('tensor'), may hold values from -0.5 to 0.5
- self_mixer_bias: bfloat16 [1024], replicated, may hold values from -1.75 to 1.75
- cross_gain: bfloat16 [1024], replicated, may hold values from 0.5 to 1.5
- cross_shift: bfloat16 [1024], replicated, may hold values from -1.75 to 1.75
- cross_query: bfloat16 [1024, 1024], P(None, 'tensor'), may hold values from -0.25 to 0.25
- cross_query_bias: bfloat16 [1024], P('tensor'), may hold values from -1.75 to 1.75
- cross_key: bfloat16 [1024, 1024], P(None, 'tensor'), may hold values from -0.1875 to 0.1875
- cross_value: bfloat16 [1024, 1024], P(None, 'tensor'), may hold values from -0.1875 to 0.1875
- cross_value_bias: bfloat16 [1024], P('tensor'), may hold values from -1.75 to 1.75
- cross_mixer: bfloat16 [1024, 1024], P('tensor'), may hold values from -0.75 to 0.75
- cross_mixer_bias: bfloat16 [1024], replicated, may hold values from -1.75 to 1.75
- feed_gain: bfloat16 [1024], replicated, may hold values from 0.5 to 1.5
- feed_shift: bfloat16 [1024], replicated, may hold values from -1.75 to 1.75
- expand_weight: bfloat16 [1024, 4096], P(None, 'tensor'), may hold values from -0.1875 to 0.1875
- expand_bias: bfloat16 [4096], P('tensor'), may hold values from -3 to 3
- reduce_weight: bfloat16 [4096, 1024], P('tensor'), may hold values from -0.125 to 0.125
- reduce_bias: bfloat16 [1024], replicated, may hold values from -1.75 to 1.75
Outputs:
- output: float32 [32, 448, 1024], P('dp')
- grad_tokens: float32 [32, 448, 1024], P('dp')
- grad_encoded: float32 [32, 1500, 1024], P('dp', None, 'tensor')
- grad_self_gain: float32 [1024], replicated
- grad_self_shift: float32 [1024], replicated
- grad_self_query: float32 [1024, 1024], P(None, 'tensor')
- grad_self_query_bias: float32 [1024], P('tensor')
- grad_self_key: float32 [1024, 1024], P(None, 'tensor')
- grad_self_value: float32 [1024, 1024], P(None, 'tensor')
- grad_self_value_bias: float32 [1024], P('tensor')
- grad_self_mixer: float32 [1024, 1024], P('tensor')
- grad_self_mixer_bias: float32 [1024], replicated
- grad_cross_gain: float32 [1024], replicated
- grad_cross_shift: float32 [1024], replicated
- grad_cross_query: float32 [1024, 1024], P(None, 'tensor')
- grad_cross_query_bias: float32 [1024], P('tensor')
- grad_cross_key: float32 [1024, 1024], P(None, 'tensor')
- grad_cross_value: float32 [1024, 1024], P(None, 'tensor')
- grad_cross_value_bias: float32 [1024], P('tensor')
- grad_cross_mixer: float32 [1024, 1024], P('tensor')
- grad_cross_mixer_bias: float32 [1024], replicated
- grad_feed_gain: float32 [1024], replicated
- grad_feed_shift: float32 [1024], replicated
- grad_expand_weight: float32 [1024, 4096], P(None, 'tensor')
- grad_expand_bias: float32 [4096], P('tensor')
- grad_reduce_weight: float32 [4096, 1024], P('tensor')
- grad_reduce_bias: float32 [1024], replicated
All inputs are finite; a program needn't handle non-finite values.
Results may differ from a plain program's by a relative error of at most 0.022.
Values may be sent and summed in bfloat16 or wider, within the bound.
No kernel may reach another device: no remote copies, remote signals or barrier semaphores. Data moves between devices by JAX's collectives and lax.ppermute only.
A program may use at most 256 MiB of HBM per device.

v0:
```python
import math
import jax
import jax.numpy as jnp
from jax import lax
from jax.sharding import PartitionSpec as P

HEAD = 64
EPSILON = 1e-05
F32 = jnp.float32
BF16 = jnp.bfloat16


def normalize(values, norm_gain, norm_shift):
    row_mean = jnp.mean(values, axis=-1, keepdims=True)
    centered = values - row_mean
    spread = jnp.mean(centered * centered, axis=-1, keepdims=True)
    inverse = lax.rsqrt(spread + EPSILON)
    normed = centered * inverse
    return (normed * norm_gain + norm_shift, normed, inverse)


def normalize_back(grad_out, normed, inverse, norm_gain):
    scaled = grad_out * norm_gain
    centre = jnp.mean(scaled, axis=-1, keepdims=True)
    row_along = jnp.mean(scaled * normed, axis=-1, keepdims=True)
    grad_in = inverse * (scaled - centre - normed * row_along)
    return (grad_in, jnp.sum(grad_out * normed, axis=0), jnp.sum(grad_out, axis=0))


def scores_of(queries, key_heads, causal):
    scaling = 1.0 / math.sqrt(queries.shape[-1])
    scores = jnp.einsum("lhe,khe->hlk", queries, key_heads, preferred_element_type=F32) * scaling
    if causal:
        row_index = lax.broadcasted_iota(jnp.int32, scores.shape[-2:], 0)
        col_index = lax.broadcasted_iota(jnp.int32, scores.shape[-2:], 1)
        scores = jnp.where(col_index <= row_index, scores, -1e30)
    return scores


def attend(queries, key_heads, value_heads, causal):
    scores = scores_of(queries, key_heads, causal)
    highest = jnp.max(scores, axis=-1, keepdims=True)
    denominator = jnp.sum(jnp.exp(scores - highest), axis=-1, keepdims=True)
    logsum = highest + jnp.log(denominator)
    probs = jnp.exp(scores - logsum)
    mixture = jnp.einsum(
        "hlk,khe->lhe", probs.astype(BF16), value_heads, preferred_element_type=F32
    )
    return (mixture.astype(BF16), logsum)


def attend_back(grad_mixture, queries, key_heads, value_heads, logsum, causal):
    scaling = 1.0 / math.sqrt(queries.shape[-1])
    probs = jnp.exp(scores_of(queries, key_heads, causal) - logsum)
    grad_probs = jnp.einsum("lhe,khe->hlk", grad_mixture, value_heads, preferred_element_type=F32)
    row_dot = jnp.sum(grad_probs * probs, axis=-1, keepdims=True)
    grad_scores = (probs * (grad_probs - row_dot)).astype(BF16)
    grad_queries = (
        jnp.einsum("hlk,khe->lhe", grad_scores, key_heads, preferred_element_type=F32) * scaling
    ).astype(BF16)
    grad_keys = (
        jnp.einsum("hlk,lhe->khe", grad_scores, queries, preferred_element_type=F32) * scaling
    ).astype(BF16)
    grad_values = jnp.einsum(
        "hlk,lhe->khe", probs.astype(BF16), grad_mixture, preferred_element_type=F32
    ).astype(BF16)
    return (grad_queries, grad_keys, grad_values)


def project(inputs, weight):
    return jnp.dot(inputs, weight, preferred_element_type=F32)


def project_back(grads, weight):
    return jnp.einsum("lc,dc->ld", grads, weight, preferred_element_type=F32)


def weight_grad(inputs, grads):
    left = jnp.concatenate(inputs, axis=0)
    right = jnp.concatenate(grads, axis=0)
    return jnp.einsum("ld,lc->dc", left, right, preferred_element_type=F32).astype(BF16)


def column_sum(grads):
    return jnp.sum(grads.astype(F32), axis=0)


def tensor_sum(partial):
    if lax.axis_size("tensor") != 2:
        return lax.psum(partial, "tensor")
    mine = lax.optimization_barrier(partial.astype(BF16))
    other = lax.ppermute(mine, "tensor", [(0, 1), (1, 0)])
    return mine.astype(F32) + other.astype(F32)


def dp_sum(grads):
    share = lax.psum_scatter(grads, "dp", scatter_dimension=0, tiled=True)
    return lax.all_gather(share, "dp", axis=0, tiled=True)


def local(
    tokens,
    encoded,
    cotangent,
    self_gain,
    self_shift,
    self_query,
    self_query_bias,
    self_key,
    self_value,
    self_value_bias,
    self_mixer,
    self_mixer_bias,
    cross_gain,
    cross_shift,
    cross_query,
    cross_query_bias,
    cross_key,
    cross_value,
    cross_value_bias,
    cross_mixer,
    cross_mixer_bias,
    feed_gain,
    feed_shift,
    expand_weight,
    expand_bias,
    reduce_weight,
    reduce_bias,
):
    clips, length, width = tokens.shape
    frames = encoded.shape[1]
    local_width = self_query.shape[1]
    head_count = local_width // HEAD
    gain_one = self_gain.astype(F32)
    gain_two = cross_gain.astype(F32)
    gain_three = feed_gain.astype(F32)
    each = range(clips)

    def heads(values):
        return values.reshape(values.shape[0], head_count, HEAD)

    def flat(values):
        return values.reshape(values.shape[0], local_width)

    source, normed_one, inverse_one, attn_in = ([], [], [], [])
    self_queries, self_keys, self_values = ([], [], [])
    self_mixture, self_logsum, self_sum = ([], [], [])
    cross_keys, cross_values = ([], [])
    for i in each:
        source.append(tokens[i].astype(F32))
        normed, plain, inverse = normalize(source[i], gain_one, self_shift.astype(F32))
        normed_one.append(plain)
        inverse_one.append(inverse)
        attn_in.append(normed.astype(BF16))
        self_queries.append(
            (project(attn_in[i], self_query) + self_query_bias.astype(F32)).astype(BF16)
        )
        self_keys.append(project(attn_in[i], self_key).astype(BF16))
        self_values.append(
            (project(attn_in[i], self_value) + self_value_bias.astype(F32)).astype(BF16)
        )
        mixed, logsum = attend(
            heads(self_queries[i]), heads(self_keys[i]), heads(self_values[i]), True
        )
        self_mixture.append(flat(mixed))
        self_logsum.append(logsum)
        self_sum.append(tensor_sum(project(self_mixture[i], self_mixer)))
    for i in each:
        cross_keys.append(project(encoded[i], cross_key).astype(BF16))
        cross_values.append(
            (project(encoded[i], cross_value) + cross_value_bias.astype(F32)).astype(BF16)
        )
    hidden_one, normed_two, inverse_two, cross_in = ([], [], [], [])
    cross_queries, cross_mixture, cross_logsum, cross_sum = ([], [], [], [])
    for i in each:
        hidden_one.append(source[i] + self_sum[i] + self_mixer_bias.astype(F32))
        normed, plain, inverse = normalize(hidden_one[i], gain_two, cross_shift.astype(F32))
        normed_two.append(plain)
        inverse_two.append(inverse)
        cross_in.append(normed.astype(BF16))
        cross_queries.append(
            (project(cross_in[i], cross_query) + cross_query_bias.astype(F32)).astype(BF16)
        )
        mixed, logsum = attend(
            heads(cross_queries[i]), heads(cross_keys[i]), heads(cross_values[i]), False
        )
        cross_mixture.append(flat(mixed))
        cross_logsum.append(logsum)
        cross_sum.append(tensor_sum(project(cross_mixture[i], cross_mixer)))
    hidden_two, normed_three, inverse_three, feed_in = ([], [], [], [])
    activated, grad_preact, feed_grad, feed_sum = ([], [], [], [])
    for i in each:
        hidden_two.append(hidden_one[i] + cross_sum[i] + cross_mixer_bias.astype(F32))
        normed, plain, inverse = normalize(hidden_two[i], gain_three, feed_shift.astype(F32))
        normed_three.append(plain)
        inverse_three.append(inverse)
        feed_in.append(normed.astype(BF16))
        preact = project(feed_in[i], expand_weight) + expand_bias.astype(F32)
        grad_activated = project_back(cotangent[i], reduce_weight)
        cdf = 0.5 * (1.0 + lax.erf(preact * (1.0 / math.sqrt(2.0))))
        density = jnp.exp(-0.5 * preact * preact) * (1.0 / math.sqrt(2.0 * math.pi))
        activated.append((preact * cdf).astype(BF16))
        grad_preact.append((grad_activated * (cdf + preact * density)).astype(BF16))
        feed_grad.append(tensor_sum(project_back(grad_preact[i], expand_weight)))
    for i in each:
        feed_sum.append(tensor_sum(project(activated[i], reduce_weight)))
    output = [hidden_two[i] + feed_sum[i] + reduce_bias.astype(F32) for i in each]
    grad_out = [cotangent[i].astype(F32) for i in each]
    grad_reduce_weight = dp_sum(weight_grad(activated, [cotangent[i] for i in each]))
    grad_expand_weight = dp_sum(weight_grad(feed_in, grad_preact))
    grad_reduce_bias = sum((jnp.sum(grad_out[i], axis=0) for i in each))
    grad_expand_bias = sum((column_sum(grad_preact[i]) for i in each))
    grad_two, two_rounded, feed_gains, feed_shifts = ([], [], [], [])
    cross_query_grad, cross_key_grad, cross_value_grad = ([], [], [])
    cross_grad = []
    for i in each:
        norm_grad, part_gain, part_shift = normalize_back(
            feed_grad[i], normed_three[i], inverse_three[i], gain_three
        )
        feed_gains.append(part_gain)
        feed_shifts.append(part_shift)
        grad_two.append(grad_out[i] + norm_grad)
        two_rounded.append(grad_two[i].astype(BF16))
        grad_cross_mixture = project_back(two_rounded[i], cross_mixer).astype(BF16)
        query_grad, key_grad, value_grad = attend_back(
            heads(grad_cross_mixture),
            heads(cross_queries[i]),
            heads(cross_keys[i]),
            heads(cross_values[i]),
            cross_logsum[i],
            False,
        )
        cross_query_grad.append(flat(query_grad))
        cross_key_grad.append(flat(key_grad))
        cross_value_grad.append(flat(value_grad))
        cross_grad.append(tensor_sum(project_back(cross_query_grad[i], cross_query)))
    grad_cross_mixer = dp_sum(weight_grad(cross_mixture, two_rounded))
    grad_cross_query = dp_sum(weight_grad(cross_in, cross_query_grad))
    frames_in = [encoded[i] for i in each]
    grad_cross_key = dp_sum(weight_grad(frames_in, cross_key_grad))
    grad_cross_value = dp_sum(weight_grad(frames_in, cross_value_grad))
    part_cross_mixer_bias = sum((jnp.sum(grad_two[i], axis=0) for i in each))
    grad_cross_query_bias = sum((column_sum(cross_query_grad[i]) for i in each))
    grad_cross_value_bias = sum((column_sum(cross_value_grad[i]) for i in each))
    grad_one, one_rounded, cross_gains, cross_shifts = ([], [], [], [])
    query_grads, key_grads, value_grads, self_grad = ([], [], [], [])
    for i in each:
        norm_grad, part_gain, part_shift = normalize_back(
            cross_grad[i], normed_two[i], inverse_two[i], gain_two
        )
        cross_gains.append(part_gain)
        cross_shifts.append(part_shift)
        grad_one.append(grad_two[i] + norm_grad)
        one_rounded.append(grad_one[i].astype(BF16))
        grad_self_mixture = project_back(one_rounded[i], self_mixer).astype(BF16)
        query_grad, key_grad, value_grad = attend_back(
            heads(grad_self_mixture),
            heads(self_queries[i]),
            heads(self_keys[i]),
            heads(self_values[i]),
            self_logsum[i],
            True,
        )
        query_grads.append(flat(query_grad))
        key_grads.append(flat(key_grad))
        value_grads.append(flat(value_grad))
        self_terms = (
            project_back(query_grads[i], self_query)
            + project_back(key_grads[i], self_key)
            + project_back(value_grads[i], self_value)
        )
        self_grad.append(tensor_sum(self_terms))
    grad_self_mixer = dp_sum(weight_grad(self_mixture, one_rounded))
    grad_self_query = dp_sum(weight_grad(attn_in, query_grads))
    grad_self_key = dp_sum(weight_grad(attn_in, key_grads))
    grad_self_value = dp_sum(weight_grad(attn_in, value_grads))
    part_self_mixer_bias = sum((jnp.sum(grad_one[i], axis=0) for i in each))
    grad_self_query_bias = sum((column_sum(query_grads[i]) for i in each))
    grad_self_value_bias = sum((column_sum(value_grads[i]) for i in each))
    grad_encoded = []
    members = lax.axis_size("tensor")
    share = width // members
    for i in each:
        if members == 2:
            me = lax.axis_index("tensor")

            def terms(part):
                rows_key = lax.dynamic_slice_in_dim(cross_key, part * share, share, 0)
                rows_value = lax.dynamic_slice_in_dim(cross_value, part * share, share, 0)
                return project_back(cross_key_grad[i], rows_key) + project_back(
                    cross_value_grad[i], rows_value
                )

            other = lax.ppermute(terms(1 - me).astype(BF16), "tensor", [(0, 1), (1, 0)])
            grad_encoded.append(terms(me) + other.astype(F32))
        else:
            frame_terms = project_back(cross_key_grad[i], cross_key) + project_back(
                cross_value_grad[i], cross_value
            )
            grad_encoded.append(
                lax.psum_scatter(frame_terms, "tensor", scatter_dimension=1, tiled=True)
            )
    self_gains, self_shifts, grad_tokens = ([], [], [])
    for i in each:
        norm_grad, part_gain, part_shift = normalize_back(
            self_grad[i], normed_one[i], inverse_one[i], gain_one
        )
        self_gains.append(part_gain)
        self_shifts.append(part_shift)
        grad_tokens.append(grad_one[i] + norm_grad)
    vectors = [
        sum(self_gains),
        sum(self_shifts),
        part_self_mixer_bias,
        sum(cross_gains),
        sum(cross_shifts),
        part_cross_mixer_bias,
        sum(feed_gains),
        sum(feed_shifts),
        grad_reduce_bias,
        grad_self_query_bias,
        grad_self_value_bias,
        grad_cross_query_bias,
        grad_cross_value_bias,
        grad_expand_bias,
    ]
    summed = lax.psum(jnp.concatenate(vectors), "dp")
    pieces, offset = ([], 0)
    for piece in vectors:
        pieces.append(summed[offset : offset + piece.size])
        offset = offset + piece.size
    return (
        jnp.stack(output),
        jnp.stack(grad_tokens),
        jnp.stack(grad_encoded),
        pieces[0],
        pieces[1],
        grad_self_query.astype(F32),
        pieces[9],
        grad_self_key.astype(F32),
        grad_self_value.astype(F32),
        pieces[10],
        grad_self_mixer.astype(F32),
        pieces[2],
        pieces[3],
        pieces[4],
        grad_cross_query.astype(F32),
        pieces[11],
        grad_cross_key.astype(F32),
        grad_cross_value.astype(F32),
        pieces[12],
        grad_cross_mixer.astype(F32),
        pieces[5],
        pieces[6],
        pieces[7],
        grad_expand_weight.astype(F32),
        pieces[13],
        grad_reduce_weight.astype(F32),
        pieces[8],
    )


def solution(mesh):
    rows = P("dp", None, None)
    column, row, part = (P(None, "tensor"), P("tensor", None), P("tensor"))
    return jax.shard_map(
        local,
        mesh=mesh,
        in_specs=(
            rows,
            rows,
            rows,
            P(),
            P(),
            column,
            part,
            column,
            column,
            part,
            row,
            P(),
            P(),
            P(),
            column,
            part,
            column,
            column,
            part,
            row,
            P(),
            P(),
            P(),
            column,
            part,
            row,
            P(),
        ),
        out_specs=(
            rows,
            rows,
            P("dp", None, "tensor"),
            P(),
            P(),
            column,
            part,
            column,
            column,
            part,
            row,
            P(),
            P(),
            P(),
            column,
            part,
            column,
            column,
            part,
            row,
            P(),
            P(),
            P(),
            column,
            part,
            row,
            P(),
        ),
        check_vma=False,
    )
```

profile of v0, /device:TPU:0, one launch (start us, length us, event | category | flops | bytes accessed | tf_op | source)
XLA Modules:
  0.0 1475.0 jit_solution(17825031323830864179)
XLA Ops:
  41.3 9.7 fusion.219
  51.0 8.1 copy_bitcast_fusion
  59.1 4.8 fusion.34
  66.4 4.8 convolution_convert_fusion.3
  81.4 4.7 multiply_reduce_fusion.3
  86.2 5.9 exponential_reduce_fusion.1
  93.5 12.3 fusion.135
  108.2 21.7 %collective-permute-done.1 = bf16[448,1024]{1,0:T(8,128)(2,1)S(1)} collective-permute-done((bf16[448,1024]{1,0:T(8,128)(2,1)S(1)}, bf16[448,1024]{1,0:T(8,128)(2,1)S(1)}, u32[]{:S(2)}, u32[]{:S(2)}) %collective-permute-start.1) | collective-permute-done | bytes 917536 | tf_op jit(solution)/shard_map/ppermute | solution.py:92
  151.8 15.1 %collective-permute-done.6 = bf16[448,1024]{1,0:T(8,128)(2,1)} collective-permute-done((bf16[448,1024]{1,0:T(8,128)(2,1)}, bf16[448,1024]{1,0:T(8,128)(2,1)}, u32[]{:S(2)}, u32[]{:S(2)}) %collective-permute-start.6) | collective-permute-done | bytes 917536 | tf_op jit(solution)/shard_map/ppermute | solution.py:92
  170.5 13.8 collective-permute-done.2
  184.3 4.5 convert_reduce_fusion.4
  194.5 15.2 %multiply_reduce_fusion.1 = (f32[8,448]{1,0:T(8,128)S(1)}, f32[8,448,1500]{2,1,0:T(8,128)}) fusion(f32[8,448,1500]{2,1,0:T(8,128)} %copy-done.1, f32[8,448]{1,0:T(8,128)S(1)} %log_add_fusion.2, bf16[448,8,64]{0,2,1:T(8,128)(2,1)} %bitcast.336, bf16[1500,8,64]{0,2,1:T(8,128)(2,1)} %bitcast.325), kind=kOutput, calls=%fused_computation.3 | convolution fusion | flops 709628416 | bytes 45031424 | tf_op jit(solution)/shard_map/lhe,khe->hlk/dot_general | solution.py:55
  209.7 15.0 %multiply_convert_fusion.1 = bf16[8,448,1500]{2,1,0:T(8,128)(2,1)S(1)} fusion(f32[8,448,1500]{2,1,0:T(8,128)} %get-tuple-element.165, f32[8,448,1500]{2,1,0:T(8,128)} %copy-done.1, f32[8,448]{1,0:T(8,128)S(1)} %get-tuple-element.164, f32[8,448]{1,0:T(8,128)S(1)} %log_add_fusion.2), kind=kLoop, calls=%fused_computation.2 | loop fusion | flops 26880000 | bytes 53788672 | tf_op jit(solution)/shard_map/convert_element_type | solution.py:57
  224.8 4.8 convert_reduce_fusion.9
  241.8 5.5 fusion.222
  247.4 5.9 collective-permute-done.7
  264.9 9.1 multiply_reduce_fusion.5
  274.7 5.3 multiply_convert_fusion.3
  291.1 5.0 fusion.35
  299.1 5.2 collective-permute-done.3
  311.9 4.2 multiply_reduce_fusion.2
  316.1 5.7 exponential_reduce_fusion
  324.0 10.1 fusion.138
  337.3 10.9 convert_reduce_fusion.3
  348.3 6.3 collective-permute-done.4
  374.0 15.8 %collective-permute-done.9 = bf16[448,1024]{1,0:T(8,128)(2,1)S(1)} collective-permute-done((bf16[448,1024]{1,0:T(8,128)(2,1)S(1)}, bf16[448,1024]{1,0:T(8,128)(2,1)S(1)}, u32[]{:S(2)}, u32[]{:S(2)}) %collective-permute-start.9) | collective-permute-done | bytes 917536 | tf_op jit(solution)/shard_map/ppermute | solution.py:92
  391.3 12.4 collective-permute-done.5
  416.4 11.9 convert_reduce_fusion.2
  429.6 5.4 fusion.113
  435.0 15.4 %multiply_reduce_fusion = (f32[8,448]{1,0:T(8,128)S(1)}, f32[8,448,1500]{2,1,0:T(8,128)}) fusion(f32[8,448,1500]{2,1,0:T(8,128)} %copy-done.2, f32[8,448]{1,0:T(8,128)S(1)} %log_add_fusion, bf16[448,8,64]{0,2,1:T(8,128)(2,1)} %bitcast.339, bf16[1500,8,64]{0,2,1:T(8,128)(2,1)} %bitcast.322), kind=kOutput, calls=%fused_computation.1 | convolution fusion | flops 709628416 | bytes 45031424 | tf_op jit(solution)/shard_map/lhe,khe->hlk/dot_general | solution.py:55
  450.9 14.9 %multiply_convert_fusion = bf16[8,448,1500]{2,1,0:T(8,128)(2,1)S(1)} fusion(f32[8,448,1500]{2,1,0:T(8,128)} %get-tuple-element.172, f32[8,448,1500]{2,1,0:T(8,128)} %copy-done.2, f32[8,448]{1,0:T(8,128)S(1)} %get-tuple-element.171, f32[8,448]{1,0:T(8,128)S(1)} %log_add_fusion), kind=kLoop, calls=%fused_computation | loop fusion | flops 26880000 | bytes 53788672 | tf_op jit(solution)/shard_map/convert_element_type | solution.py:57
  473.7 5.4 fusion.110
  479.2 8.1 convert_reduce_fusion.8
  490.6 5.9 convert_reduce_fusion.11
  499.3 6.6 collective-permute-done.10
  513.9 5.3 convert_reduce_fusion.10
  528.0 4.7 multiply_reduce_fusion.4
  532.7 4.2 multiply_convert_fusion.2
  552.2 6.2 convolution_convert_fusion
  559.8 8.2 convolution_convert_fusion.1
  569.4 23.4 %reduce-scatter.21.cloned.1.call-done = bf16[64,512]{1,0:T(8,128)(2,1)} async-done(((bf16[1024,512]{1,0:T(8,128)(2,1)}), bf16[64,512]{1,0:T(8,128)(2,1)}) %reduce-scatter.21.cloned.1.call-update) | async-done | bytes 65552 | tf_op jit(solution)/shard_map/reduce_scatter | solution.py:97
  592.8 60.1 %reduce-scatter.19.cloned.1.call-done = bf16[64,512]{1,0:T(8,128)(2,1)} async-done(((bf16[1024,512]{1,0:T(8,128)(2,1)}), bf16[64,512]{1,0:T(8,128)(2,1)}) %reduce-scatter.19.cloned.1.call-update) | async-done | bytes 65552 | tf_op jit(solution)/shard_map/reduce_scatter | solution.py:97
  652.9 60.1 %reduce-scatter.15.cloned.1.call-done = bf16[64,512]{1,0:T(8,128)(2,1)} async-done(((bf16[1024,512]{1,0:T(8,128)(2,1)}), bf16[64,512]{1,0:T(8,128)(2,1)}) %reduce-scatter.15.cloned.1.call-update) | async-done | bytes 65552 | tf_op jit(solution)/shard_map/reduce_scatter | solution.py:97
  713.1 60.1 %reduce-scatter.17.cloned.1.call-done = bf16[32,1024]{1,0:T(8,128)(2,1)} async-done(((bf16[512,1024]{1,0:T(8,128)(2,1)}), bf16[32,1024]{1,0:T(8,128)(2,1)}) %reduce-scatter.17.cloned.1.call-update) | async-done | bytes 65552 | tf_op jit(solution)/shard_map/reduce_scatter | solution.py:97
  773.2 60.8 %reduce-scatter.11.cloned.1.call-done = bf16[64,512]{1,0:T(8,128)(2,1)} async-done(((bf16[1024,512]{1,0:T(8,128)(2,1)}), bf16[64,512]{1,0:T(8,128)(2,1)}) %reduce-scatter.11.cloned.1.call-update) | async-done | bytes 65552 | tf_op jit(solution)/shard_map/reduce_scatter | solution.py:97
  834.1 60.7 %reduce-scatter.13.cloned.1.call-done = bf16[64,512]{1,0:T(8,128)(2,1)} async-done(((bf16[1024,512]{1,0:T(8,128)(2,1)}), bf16[64,512]{1,0:T(8,128)(2,1)}) %reduce-scatter.13.cloned.1.call-update) | async-done | bytes 65552 | tf_op jit(solution)/shard_map/reduce_scatter | solution.py:97
  894.9 76.2 %reduce-scatter.29.cloned.1.call-done = bf16[128,1024]{1,0:T(8,128)(2,1)} async-done(((bf16[2048,1024]{1,0:T(8,128)(2,1)}), bf16[128,1024]{1,0:T(8,128)(2,1)}) %reduce-scatter.29.cloned.1.call-update) | async-done | bytes 262160 | tf_op jit(solution)/shard_map/reduce_scatter | solution.py:97
  983.4 29.0 %collective-permute-done.12 = bf16[1500,512]{1,0:T(8,128)(2,1)} collective-permute-done((bf16[1500,512]{1,0:T(8,128)(2,1)}, bf16[1500,512]{1,0:T(8,128)(2,1)}, u32[]{:S(2)}, u32[]{:S(2)}) %collective-permute-start.12) | collective-permute-done | bytes 1536032 | tf_op jit(solution)/shard_map/ppermute | solution.py:294
  1012.4 4.2 add_bitcast_fusion.1
  1019.2 28.0 %reduce-scatter.27.cloned.1.call-done = bf16[64,2048]{1,0:T(8,128)(2,1)} async-done(((bf16[1024,2048]{1,0:T(8,128)(2,1)}), bf16[64,2048]{1,0:T(8,128)(2,1)}) %reduce-scatter.27.cloned.1.call-update) | async-done | bytes 262160 | tf_op jit(solution)/shard_map/reduce_scatter | solution.py:97
  1047.3 4.7 fusion.37
  1063.9 25.0 %collective-permute-done.13 = bf16[1500,512]{1,0:T(8,128)(2,1)} collective-permute-done((bf16[1500,512]{1,0:T(8,128)(2,1)}, bf16[1500,512]{1,0:T(8,128)(2,1)}, u32[]{:S(2)}, u32[]{:S(2)}) %collective-permute-start.13) | collective-permute-done | bytes 1536032 | tf_op jit(solution)/shard_map/ppermute | solution.py:294
  1093.7 12.7 copy.122
  1106.5 4.0 fusion.70
  1110.9 57.9 %psum.7 = f32[13312]{0:T(1024)S(1)} all-reduce(f32[13312]{0:T(1024)S(1)} %add_dynamic-update-slice_fusion), channel_id=1, replica_groups=mesh['dp'=16,'tensor'=2] {'dp'}, use_global_device_ids=true, to_apply=%region_64.65 | all-reduce | flops 13312 | bytes 106496 | tf_op jit(solution)/shard_map/psum | solution.py:327
  1185.3 17.9 %all-gather.19.cloned.1.call-done = bf16[1024,512]{1,0:T(8,128)(2,1)} async-done(((bf16[64,512]{1,0:T(8,128)(2,1)}), bf16[1024,512]{1,0:T(8,128)(2,1)}) %all-gather.19.cloned.1.call-update) | async-done | bytes 1048592 | tf_op jit(solution)/shard_map/all_gather | solution.py:98
  1206.1 36.0 %all-gather.15.cloned.1.call-done = bf16[1024,512]{1,0:T(8,128)(2,1)} async-done(((bf16[64,512]{1,0:T(8,128)(2,1)}), bf16[1024,512]{1,0:T(8,128)(2,1)}) %all-gather.15.cloned.1.call-update) | async-done | bytes 1048592 | tf_op jit(solution)/shard_map/all_gather | solution.py:98
  1245.0 36.0 %all-gather.17.cloned.1.call-done = bf16[512,1024]{1,0:T(8,128)(2,1)} async-done(((bf16[32,1024]{1,0:T(8,128)(2,1)}), bf16[512,1024]{1,0:T(8,128)(2,1)}) %all-gather.17.cloned.1.call-update) | async-done | bytes 1048592 | tf_op jit(solution)/shard_map/all_gather | solution.py:98
  1283.8 36.1 %all-gather.11.cloned.1.call-done = bf16[1024,512]{1,0:T(8,128)(2,1)} async-done(((bf16[64,512]{1,0:T(8,128)(2,1)}), bf16[1024,512]{1,0:T(8,128)(2,1)}) %all-gather.11.cloned.1.call-update) | async-done | bytes 1048592 | tf_op jit(solution)/shard_map/all_gather | solution.py:98
  1322.8 36.0 %all-gather.13.cloned.1.call-done = bf16[1024,512]{1,0:T(8,128)(2,1)} async-done(((bf16[64,512]{1,0:T(8,128)(2,1)}), bf16[1024,512]{1,0:T(8,128)(2,1)}) %all-gather.13.cloned.1.call-update) | async-done | bytes 1048592 | tf_op jit(solution)/shard_map/all_gather | solution.py:98
  1361.6 48.7 %all-gather.29.cloned.1.call-done = bf16[2048,1024]{1,0:T(8,128)(2,1)} async-done(((bf16[128,1024]{1,0:T(8,128)(2,1)}), bf16[2048,1024]{1,0:T(8,128)(2,1)}) %all-gather.29.cloned.1.call-update) | async-done | bytes 4194320 | tf_op jit(solution)/shard_map/all_gather | solution.py:98
  1410.3 6.6 convert_element_type.662
  1417.0 44.3 %all-gather.27.cloned.1.call-done = bf16[1024,2048]{1,0:T(8,128)(2,1)} async-done(((bf16[64,2048]{1,0:T(8,128)(2,1)}), bf16[1024,2048]{1,0:T(8,128)(2,1)}) %all-gather.27.cloned.1.call-update) | async-done | bytes 4194320 | tf_op jit(solution)/shard_map/all_gather | solution.py:98
  1461.3 6.7 convert_element_type.660
  (591 shorter events, 279.0 us)
Async XLA Ops:
  7.2 59.2 %copy-start = (bf16[1024,512]{1,0:T(8,128)(2,1)S(1)}, bf16[1024,512]{1,0:T(8,128)(2,1)}, u32[]{:S(2)}) copy-start(bf16[1024,512]{1,0:T(8,128)(2,1)} %param.43) | copy-start | bytes 3145732
  7.2 560.9 %reduce-scatter.25.cloned.1.call-start = ((), (), s32[]{:S(2)}) async-start(), calls=%async_computation.24 | async-start | bytes 1114112 | tf_op jit(solution)/shard_map/reduce_scatter | solution.py:97
  36.5 14.5 copy-start.155
  38.2 35.6 %collective-permute-start = (bf16[448,1024]{1,0:T(8,128)(2,1)}, bf16[448,1024]{1,0:T(8,128)(2,1)}, u32[]{:S(2)}, u32[]{:S(2)}) collective-permute-start(bf16[448,1024]{1,0:T(8,128)(2,1)} %convolution_convert_fusion.14), channel_id=1, source_target_pairs={{0,1},{1,0},{2,3},{3,2},{4,5},{5,4},{6,7},{7,6},{8,9},{9,8},{10,11... | collective-permute-start | bytes 2752520 | tf_op jit(solution)/shard_map/ppermute | solution.py:92
  105.9 24.1 %copy-start.11 = (f32[448,1024]{1,0:T(8,128)S(1)}, f32[448,1024]{1,0:T(8,128)}, u32[]{:S(2)}) copy-start(f32[448,1024]{1,0:T(8,128)} %copy-done.10) | copy-start | bytes 5505028
  108.1 21.9 %collective-permute-start.1 = (bf16[448,1024]{1,0:T(8,128)(2,1)S(1)}, bf16[448,1024]{1,0:T(8,128)(2,1)S(1)}, u32[]{:S(2)}, u32[]{:S(2)}) collective-permute-start(bf16[448,1024]{1,0:T(8,128)(2,1)S(1)} %convolution_convert_fusion.13), channel_id=1, source_target_pairs={{0,1},{1,0},{2,3},{3,2},{4,5},{5,4},{6,7},{7,6},{8,9},{9,8},{10,11... | collective-permute-start | bytes 2752520 | tf_op jit(solution)/shard_map/ppermute | solution.py:92
  143.3 23.5 %collective-permute-start.6 = (bf16[448,1024]{1,0:T(8,128)(2,1)}, bf16[448,1024]{1,0:T(8,128)(2,1)}, u32[]{:S(2)}, u32[]{:S(2)}) collective-permute-start(bf16[448,1024]{1,0:T(8,128)(2,1)} %convolution_convert_fusion.16), channel_id=1, source_target_pairs={{0,1},{1,0},{2,3},{3,2},{4,5},{5,4},{6,7},{7,6},{8,9},{9,8},{10,11... | collective-permute-start | bytes 2752520 | tf_op jit(solution)/shard_map/ppermute | solution.py:92
  146.6 37.6 %collective-permute-start.2 = (bf16[448,1024]{1,0:T(8,128)(2,1)}, bf16[448,1024]{1,0:T(8,128)(2,1)}, u32[]{:S(2)}, u32[]{:S(2)}) collective-permute-start(bf16[448,1024]{1,0:T(8,128)(2,1)} %convolution_convert_fusion.18), channel_id=1, source_target_pairs={{0,1},{1,0},{2,3},{3,2},{4,5},{5,4},{6,7},{7,6},{8,9},{9,8},{10,11... | collective-permute-start | bytes 2752520 | tf_op jit(solution)/shard_map/ppermute | solution.py:92
  151.8 32.5 %copy-start.14 = (f32[448,1024]{1,0:T(8,128)S(1)}, f32[448,1024]{1,0:T(8,128)}, u32[]{:S(2)}) copy-start(f32[448,1024]{1,0:T(8,128)} %copy-done.13) | copy-start | bytes 5505028
  151.8 32.5 %copy-start.37 = (bf16[2,448,1024]{2,1,0:T(8,128)(2,1)S(1)}, bf16[2,448,1024]{2,1,0:T(8,128)(2,1)}, u32[]{:S(2)}) copy-start(bf16[2,448,1024]{2,1,0:T(8,128)(2,1)} %param.29) | copy-start | bytes 5505028
  209.7 15.0 %copy-start.22 = (bf16[1500,512]{0,1:T(8,128)(2,1)S(1)}, bf16[1500,512]{0,1:T(8,128)(2,1)}, u32[]{:S(2)}) copy-start(bf16[1500,512]{0,1:T(8,128)(2,1)} %copy.103) | copy-start | bytes 4608004
  232.9 20.4 %collective-permute-start.7 = (bf16[448,1024]{1,0:T(8,128)(2,1)}, bf16[448,1024]{1,0:T(8,128)(2,1)}, u32[]{:S(2)}, u32[]{:S(2)}) collective-permute-start(bf16[448,1024]{1,0:T(8,128)(2,1)} %convolution_convert_fusion.10), channel_id=1, source_target_pairs={{0,1},{1,0},{2,3},{3,2},{4,5},{5,4},{6,7},{7,6},{8,9},{9,8},{10,11... | collective-permute-start | bytes 2752520 | tf_op jit(solution)/shard_map/ppermute | solution.py:92
  241.8 11.5 copy-start.12
  247.4 9.0 copy-start.28
  264.9 9.1 slice-start
  264.9 9.1 slice-start.2
  264.9 9.1 slice-start.1
  264.9 9.7 slice-start.3
  284.8 19.5 %collective-permute-start.3 = (bf16[448,1024]{1,0:T(8,128)(2,1)}, bf16[448,1024]{1,0:T(8,128)(2,1)}, u32[]{:S(2)}, u32[]{:S(2)}) collective-permute-start(bf16[448,1024]{1,0:T(8,128)(2,1)} %convolution_convert_fusion.12), channel_id=1, source_target_pairs={{0,1},{1,0},{2,3},{3,2},{4,5},{5,4},{6,7},{7,6},{8,9},{9,8},{10,11... | collective-permute-start | bytes 2752520 | tf_op jit(solution)/shard_map/ppermute | solution.py:92
  336.2 18.5 %copy-start.9 = (f32[448,1024]{1,0:T(8,128)S(1)}, f32[448,1024]{1,0:T(8,128)}, u32[]{:S(2)}) copy-start(f32[448,1024]{1,0:T(8,128)} %copy-done.8) | copy-start | bytes 5505028
  336.2 18.4 %collective-permute-start.4 = (bf16[448,1024]{1,0:T(8,128)(2,1)S(1)}, bf16[448,1024]{1,0:T(8,128)(2,1)S(1)}, u32[]{:S(2)}, u32[]{:S(2)}) collective-permute-start(bf16[448,1024]{1,0:T(8,128)(2,1)S(1)} %convolution_convert_fusion.11), channel_id=1, source_target_pairs={{0,1},{1,0},{2,3},{3,2},{4,5},{5,4},{6,7},{7,6},{8,9},{9,8},{10,11... | collective-permute-start | bytes 2752520 | tf_op jit(solution)/shard_map/ppermute | solution.py:92
  366.5 23.3 %collective-permute-start.9 = (bf16[448,1024]{1,0:T(8,128)(2,1)S(1)}, bf16[448,1024]{1,0:T(8,128)(2,1)S(1)}, u32[]{:S(2)}, u32[]{:S(2)}) collective-permute-start(bf16[448,1024]{1,0:T(8,128)(2,1)S(1)} %convolution_convert_fusion.15), channel_id=1, source_target_pairs={{0,1},{1,0},{2,3},{3,2},{4,5},{5,4},{6,7},{7,6},{8,9},{9,8},{10,11... | collective-permute-start | bytes 2752520 | tf_op jit(solution)/shard_map/ppermute | solution.py:92
  370.0 33.7 %collective-permute-start.5 = (bf16[448,1024]{1,0:T(8,128)(2,1)S(1)}, bf16[448,1024]{1,0:T(8,128)(2,1)S(1)}, u32[]{:S(2)}, u32[]{:S(2)}) collective-permute-start(bf16[448,1024]{1,0:T(8,128)(2,1)S(1)} %convolution_convert_fusion.17), channel_id=1, source_target_pairs={{0,1},{1,0},{2,3},{3,2},{4,5},{5,4},{6,7},{7,6},{8,9},{9,8},{10,11... | collective-permute-start | bytes 2752520 | tf_op jit(solution)/shard_map/ppermute | solution.py:92
  414.1 154.7 %reduce-scatter.23.cloned.1.call-start = ((), (), s32[]{:S(2)}) async-start(), calls=%async_computation.22 | async-start | bytes 1114112 | tf_op jit(solution)/shard_map/reduce_scatter | solution.py:97
  416.4 13.1 copy-start.30
  416.4 13.1 copy-start.62
  416.4 13.1 copy-start.64
  450.4 142.3 %reduce-scatter.21.cloned.1.call-start = ((), (), s32[]{:S(2)}) async-start(), calls=%async_computation.20 | async-start | bytes 1114112 | tf_op jit(solution)/shard_map/reduce_scatter | solution.py:97
  450.9 15.0 %copy-start.41 = (bf16[448,512]{0,1:T(8,128)(2,1)S(1)}, bf16[448,512]{0,1:T(8,128)(2,1)}, u32[]{:S(2)}) copy-start(bf16[448,512]{0,1:T(8,128)(2,1)} %copy.110) | copy-start | bytes 1376260
  479.1 173.8 %reduce-scatter.19.cloned.1.call-start = ((), (), s32[]{:S(2)}) async-start(), calls=%async_computation.18 | async-start | bytes 1114112 | tf_op jit(solution)/shard_map/reduce_scatter | solution.py:97
  489.0 16.9 %collective-permute-start.10 = (bf16[448,1024]{1,0:T(8,128)(2,1)}, bf16[448,1024]{1,0:T(8,128)(2,1)}, u32[]{:S(2)}, u32[]{:S(2)}) collective-permute-start(bf16[448,1024]{1,0:T(8,128)(2,1)} %convolution_convert_fusion.9), channel_id=1, source_target_pairs={{0,1},{1,0},{2,3},{3,2},{4,5},{5,4},{6,7},{7,6},{8,9},{9,8},{10,11... | collective-permute-start | bytes 2752520 | tf_op jit(solution)/shard_map/ppermute | solution.py:92
  499.1 214.0 %reduce-scatter.15.cloned.1.call-start = ((), (), s32[]{:S(2)}) async-start(), calls=%async_computation.14 | async-start | bytes 1114112 | tf_op jit(solution)/shard_map/reduce_scatter | solution.py:97
  499.3 9.1 copy-start.26
  522.5 250.7 %reduce-scatter.17.cloned.1.call-start = ((), (), s32[]{:S(2)}) async-start(), calls=%async_computation.16 | async-start | bytes 1114112 | tf_op jit(solution)/shard_map/reduce_scatter | solution.py:97
  525.6 13.2 copy-start.73
  527.9 306.1 %reduce-scatter.11.cloned.1.call-start = ((), (), s32[]{:S(2)}) async-start(), calls=%async_computation.10 | async-start | bytes 1114112 | tf_op jit(solution)/shard_map/reduce_scatter | solution.py:97
  542.2 352.6 %reduce-scatter.13.cloned.1.call-start = ((), (), s32[]{:S(2)}) async-start(), calls=%async_computation.12 | async-start | bytes 1114112 | tf_op jit(solution)/shard_map/reduce_scatter | solution.py:97
  550.0 421.1 %reduce-scatter.29.cloned.1.call-start = ((), (), s32[]{:S(2)}) async-start(), calls=%async_computation.28 | async-start | bytes 4456448 | tf_op jit(solution)/shard_map/reduce_scatter | solution.py:97
  558.4 488.8 %reduce-scatter.27.cloned.1.call-start = ((), (), s32[]{:S(2)}) async-start(), calls=%async_computation.26 | async-start | bytes 4456448 | tf_op jit(solution)/shard_map/reduce_scatter | solution.py:97
  568.0 403.6 %copy-start.18 = (bf16[8,64,1500]{2,1,0:T(8,128)(2,1)S(1)}, bf16[8,64,1500]{2,1,0:T(8,128)(2,1)}, u32[]{:S(2)}) copy-start(bf16[8,64,1500]{2,1,0:T(8,128)(2,1)} %fusion.32) | copy-start | bytes 4608004
  568.0 608.8 %all-gather.25.cloned.1.call-start = ((), (), s32[]{:S(2)}) async-start(), calls=%async_computation.25 | async-start | bytes 1114112 | tf_op jit(solution)/shard_map/all_gather | solution.py:98
  568.8 610.9 %all-gather.23.cloned.1.call-start = ((), (), s32[]{:S(2)}) async-start(), calls=%async_computation.23 | async-start | bytes 1114112 | tf_op jit(solution)/shard_map/all_gather | solution.py:98
  569.3 613.2 %all-gather.21.cloned.1.call-start = ((), (), s32[]{:S(2)}) async-start(), calls=%async_computation.21 | async-start | bytes 1114112 | tf_op jit(solution)/shard_map/all_gather | solution.py:98
  592.8 610.5 %all-gather.19.cloned.1.call-start = ((), (), s32[]{:S(2)}) async-start(), calls=%async_computation.19 | async-start | bytes 1114112 | tf_op jit(solution)/shard_map/all_gather | solution.py:98
  652.9 589.3 %all-gather.15.cloned.1.call-start = ((), (), s32[]{:S(2)}) async-start(), calls=%async_computation.15 | async-start | bytes 1114112 | tf_op jit(solution)/shard_map/all_gather | solution.py:98
  713.0 568.0 %all-gather.17.cloned.1.call-start = ((), (), s32[]{:S(2)}) async-start(), calls=%async_computation.17 | async-start | bytes 1114112 | tf_op jit(solution)/shard_map/all_gather | solution.py:98
  773.2 546.7 %all-gather.11.cloned.1.call-start = ((), (), s32[]{:S(2)}) async-start(), calls=%async_computation.11 | async-start | bytes 1114112 | tf_op jit(solution)/shard_map/all_gather | solution.py:98
  834.0 524.8 %all-gather.13.cloned.1.call-start = ((), (), s32[]{:S(2)}) async-start(), calls=%async_computation.13 | async-start | bytes 1114112 | tf_op jit(solution)/shard_map/all_gather | solution.py:98
  894.8 515.5 %all-gather.29.cloned.1.call-start = ((), (), s32[]{:S(2)}) async-start(), calls=%async_computation.29 | async-start | bytes 4456448 | tf_op jit(solution)/shard_map/all_gather | solution.py:98
  971.1 490.2 %all-gather.27.cloned.1.call-start = ((), (), s32[]{:S(2)}) async-start(), calls=%async_computation.27 | async-start | bytes 4456448 | tf_op jit(solution)/shard_map/all_gather | solution.py:98
  975.5 36.9 %collective-permute-start.12 = (bf16[1500,512]{1,0:T(8,128)(2,1)}, bf16[1500,512]{1,0:T(8,128)(2,1)}, u32[]{:S(2)}, u32[]{:S(2)}) collective-permute-start(bf16[1500,512]{1,0:T(8,128)(2,1)} %fusion.36), channel_id=1, source_target_pairs={{0,1},{1,0},{2,3},{3,2},{4,5},{5,4},{6,7},{7,6},{8,9},{9,8},{10,11... | collective-permute-start | bytes 4608008 | tf_op jit(solution)/shard_map/ppermute | solution.py:294
  981.1 31.3 %copy-start.32 = (bf16[8,64,1500]{2,1,0:T(8,128)(2,1)S(1)}, bf16[8,64,1500]{2,1,0:T(8,128)(2,1)}, u32[]{:S(2)}) copy-start(bf16[8,64,1500]{2,1,0:T(8,128)(2,1)} %get-tuple-element.188) | copy-start | bytes 4608004
  981.1 31.3 %copy-start.60 = (bf16[1024,512]{1,0:T(8,128)(2,1)S(1)}, bf16[1024,512]{1,0:T(8,128)(2,1)}, u32[]{:S(2)}) copy-start(bf16[1024,512]{1,0:T(8,128)(2,1)} %param.44) | copy-start | bytes 3145732
  982.8 33.7 %copy-start.20 = (bf16[8,64,1500]{2,1,0:T(8,128)(2,1)S(1)}, bf16[8,64,1500]{2,1,0:T(8,128)(2,1)}, u32[]{:S(2)}) copy-start(bf16[8,64,1500]{2,1,0:T(8,128)(2,1)} %copy-done.19) | copy-start | bytes 4608004
  982.8 123.6 %collective-permute-start.8 = (bf16[448,1024]{1,0:T(8,128)(2,1)}, bf16[448,1024]{1,0:T(8,128)(2,1)}, u32[]{:S(2)}, u32[]{:S(2)}) collective-permute-start(bf16[448,1024]{1,0:T(8,128)(2,1)} %add_convert_fusion.1), channel_id=1, source_target_pairs={{0,1},{1,0},{2,3},{3,2},{4,5},{5,4},{6,7},{7,6},{8,9},{9,8},{10,11... | collective-permute-start | bytes 2752520 | tf_op jit(solution)/shard_map/ppermute | solution.py:92
  1052.0 36.9 %collective-permute-start.13 = (bf16[1500,512]{1,0:T(8,128)(2,1)}, bf16[1500,512]{1,0:T(8,128)(2,1)}, u32[]{:S(2)}, u32[]{:S(2)}) collective-permute-start(bf16[1500,512]{1,0:T(8,128)(2,1)} %fusion.37), channel_id=1, source_target_pairs={{0,1},{1,0},{2,3},{3,2},{4,5},{5,4},{6,7},{7,6},{8,9},{9,8},{10,11... | collective-permute-start | bytes 4608008 | tf_op jit(solution)/shard_map/ppermute | solution.py:294
  1060.7 45.8 %collective-permute-start.11 = (bf16[448,1024]{1,0:T(8,128)(2,1)}, bf16[448,1024]{1,0:T(8,128)(2,1)}, u32[]{:S(2)}, u32[]{:S(2)}) collective-permute-start(bf16[448,1024]{1,0:T(8,128)(2,1)} %add_convert_fusion), channel_id=1, source_target_pairs={{0,1},{1,0},{2,3},{3,2},{4,5},{5,4},{6,7},{7,6},{8,9},{9,8},{10,11... | collective-permute-start | bytes 2752520 | tf_op jit(solution)/shard_map/ppermute | solution.py:92
  1061.3 27.6 %copy-start.34 = (bf16[8,64,1500]{2,1,0:T(8,128)(2,1)S(1)}, bf16[8,64,1500]{2,1,0:T(8,128)(2,1)}, u32[]{:S(2)}) copy-start(bf16[8,64,1500]{2,1,0:T(8,128)(2,1)} %copy-done.33) | copy-start | bytes 4608004
  1093.6 12.9 copy-start.7
  1093.6 12.9 copy-start.109
  1093.6 12.9 copy-start.111
  1093.6 12.9 copy-start.113
  1093.7 12.9 copy-start.115
  1093.7 12.9 copy-start.117
  (144 other events, 470.6 us)
Sparse Core Ops, SparseCore 0:
  414.3 57.9 reduce-scatter.24
  475.8 56.7 reduce-scatter.22
  536.3 56.4 reduce-scatter.20
  596.2 56.6 reduce-scatter.18
  656.3 56.6 reduce-scatter.14
  716.5 56.6 reduce-scatter.16
  777.4 56.6 reduce-scatter.10
  838.2 56.5 reduce-scatter.12
  899.2 71.8 reduce-scatter.28
  975.4 71.8 reduce-scatter.26
  1049.4 36.9 all-gather.24
  1088.4 36.8 all-gather.22
  1127.5 36.8 all-gather.20
  1166.4 36.7 all-gather.18
  1205.3 36.8 all-gather.14
  1244.2 36.8 all-gather.16
  1283.1 36.8 all-gather.10
  1321.9 36.8 all-gather.12
  1361.0 49.3 all-gather.28
  1412.4 48.8 all-gather.26
where the time goes:
time: 1480 us; the launch traced here: 1470 us
  waiting for transfers between devices  843 us (57%)
  matrix products  294 us (20%)
  other arithmetic  140 us (9%)
  local copies, waits for them, and re-layouts  105 us (7%)
  blocking collectives  57.9 us (4%)
  starting transfers between devices  17.7 us (1%)
  between operations  16.5 us (1%)
    reduce_scatter x10, waiting for transfers between devices, dp_sum(): share = lax.psum_scatter(grads, 'dp', scatter_dimension=0, tiled=True)  429 us
    all_gather x10, waiting for transfers between devices, dp_sum(): return lax.all_gather(share, 'dp', axis=0, tiled=True)  255 us
    ppermute x12, waiting for transfers between devices, tensor_sum(): other = lax.ppermute(mine, 'tensor', [(0, 1), (1, 0)])  103 us
    psum x1, blocking collectives, local(): summed = lax.psum(jnp.concatenate(vectors), 'dp')  57.9 us
    ppermute x2, waiting for transfers between devices, local(): other = lax.ppermute(terms(1 - me).astype(BF16), 'tensor', [(0, 1), (1, 0)])  54 us
    dot_general x24, matrix products, project_back(): return jnp.einsum('lc,dc->ld', grads, weight, preferred_element_type=F32)  53.9 us
    unnamed x353, local copies, waits for them, and re-layouts  52.1 us
    dot_general x20, matrix products, project(): return jnp.dot(inputs, weight, preferred_element_type=F32)  51.3 us
  transfers between devices with their start and end apart: 34, of which 26 were waited for; matrix products, arithmetic and copies ran while one was open for 20% of the time, Pallas kernels for 0%

commit v1 on v0

--- a/solution.py
+++ b/solution.py
@@ -8,6 +8,19 @@
 EPSILON = 1e-05
 F32 = jnp.float32
 BF16 = jnp.bfloat16
+
+
+def ring_gather(array, axis, dim):
+    ways = lax.axis_size(axis)
+    up = [(d, (d + 1) % ways) for d in range(ways)]
+    down = [(d, (d - 1) % ways) for d in range(ways)]
+    earlier, later = ([array], [array])
+    for _ in range(ways // 2):
+        earlier.append(lax.ppermute(earlier[-1], axis, up))
+    for _ in range((ways - 1) // 2):
+        later.append(lax.ppermute(later[-1], axis, down))
+    line = jnp.concatenate([*earlier[::-1], *later[1:]], axis=dim)
+    return jnp.roll(line, (lax.axis_index(axis) - ways // 2) * array.shape[dim], axis=dim)
 
 
 def normalize(values, norm_gain, norm_shift):
@@ -95,7 +108,7 @@
 
 def dp_sum(grads):
     share = lax.psum_scatter(grads, "dp", scatter_dimension=0, tiled=True)
-    return lax.all_gather(share, "dp", axis=0, tiled=True)
+    return ring_gather(share, "dp", 0)
 
 
 def local(

time: 1480 us -> 1220 us (0.82)
  waiting for transfers between devices: 843 us -> 301 us
  starting transfers between devices: 17.7 us -> 228 us
  local copies, waits for them, and re-layouts: 105 us -> 150 us
    reduce_scatter x10, waiting for transfers between devices: 429 us -> 63.7 us  [dp_sum(): share = lax.psum_scatter(grads, 'dp', scatter_dimension=0, tiled=True)]
    all_gather x10 -> x0, waiting for transfers between devices: 255 us -> none  [dp_sum(): return lax.all_gather(share, 'dp', axis=0, tiled=True)]
    ppermute x0 -> x150, starting transfers between devices: none -> 210 us  [the longest x70 182 us: ring_gather(): later.append(lax.ppermute(later[-1], axis, down))]
    ppermute x0 -> x150, waiting for transfers between devices: none -> 87.8 us  [the longest x80 80.4 us: ring_gather(): earlier.append(lax.ppermute(earlier[-1], axis, up))]
    unnamed x353 -> x547, local copies, waits for them, and re-layouts: 52.1 us -> 92.7 us
  transfers between devices with their start and end apart: 34 -> 174, of which waited for: 26 -> 48; matrix products, arithmetic and copies ran while one was open for 20% -> 28% of each run, Pallas kernels for 0% -> 0%
where the time goes in v1:
time: 1220 us; the launch traced here: 1200 us
  waiting for transfers between devices  301 us (25%)
  matrix products  294 us (24%)
  starting transfers between devices  228 us (19%)
  local copies, waits for them, and re-layouts  150 us (12%)
  other arithmetic  150 us (12%)
  blocking collectives  62.8 us (5%)
  between operations  17.8 us (1%)
    ppermute x70, starting transfers between devices, ring_gather(): later.append(lax.ppermute(later[-1], axis, down))  182 us
    ppermute x12, waiting for transfers between devices, tensor_sum(): other = lax.ppermute(mine, 'tensor', [(0, 1), (1, 0)])  99.5 us
    unnamed x547, local copies, waits for them, and re-layouts  92.7 us
    ppermute x80, waiting for transfers between devices, ring_gather(): earlier.append(lax.ppermute(earlier[-1], axis, up))  80.4 us
    reduce_scatter x10, waiting for transfers between devices, dp_sum(): share = lax.psum_scatter(grads, 'dp', scatter_dimension=0, tiled=True)  63.7 us
    psum x1, blocking collectives, local(): summed = lax.psum(jnp.concatenate(vectors), 'dp')  62.8 us
    dot_general x20, matrix products, project(): return jnp.dot(inputs, weight, preferred_element_type=F32)  52.5 us
    ppermute x2, waiting for transfers between devices, local(): other = lax.ppermute(terms(1 - me).astype(BF16), 'tensor', [(0, 1), (1, 0)])  50 us
  transfers between devices with their start and end apart: 174, of which 48 were waited for; matrix products, arithmetic and copies ran while one was open for 28% of the time, Pallas kernels for 0%

profile of v1, /device:TPU:0, one launch (start us, length us, event | category | flops | bytes accessed | tf_op | source)
XLA Modules:
  0.0 1203.9 jit_solution(8123947879602824000)
XLA Ops:
  41.3 9.7 fusion.235
  51.0 8.0 copy_bitcast_fusion
  59.1 4.8 fusion.34
  66.4 4.8 convolution_convert_fusion.3
  81.7 4.7 multiply_reduce_fusion.3
  86.4 5.9 exponential_reduce_fusion.1
  93.8 12.3 %fusion.135 = bf16[8,64,448]{2,1,0:T(8,128)(2,1)} fusion(bf16[1500,8,64]{0,2,1:T(8,128)(2,1)} %bitcast.324, f32[8,448,1500]{2,1,0:T(8,128)} %copy-done.1, f32[8,448]{1,0:T(8,128)S(1)} %log_add_fusion.2), kind=kOutput, calls=%fused_computation.259 | convolution fusion | flops 704485376 | bytes 23513088 | tf_op jit(solution)/shard_map/hlk,khe->lhe/dot_general | solution.py:59
  108.4 21.7 %collective-permute-done.1 = bf16[448,1024]{1,0:T(8,128)(2,1)S(1)} collective-permute-done((bf16[448,1024]{1,0:T(8,128)(2,1)S(1)}, bf16[448,1024]{1,0:T(8,128)(2,1)S(1)}, u32[]{:S(2)}, u32[]{:S(2)}) %collective-permute-start.1) | collective-permute-done | bytes 917536 | tf_op jit(solution)/shard_map/ppermute | solution.py:105
  152.0 15.1 %collective-permute-done.6 = bf16[448,1024]{1,0:T(8,128)(2,1)} collective-permute-done((bf16[448,1024]{1,0:T(8,128)(2,1)}, bf16[448,1024]{1,0:T(8,128)(2,1)}, u32[]{:S(2)}, u32[]{:S(2)}) %collective-permute-start.6) | collective-permute-done | bytes 917536 | tf_op jit(solution)/shard_map/ppermute | solution.py:105
  170.7 13.8 %collective-permute-done.2 = bf16[448,1024]{1,0:T(8,128)(2,1)} collective-permute-done((bf16[448,1024]{1,0:T(8,128)(2,1)}, bf16[448,1024]{1,0:T(8,128)(2,1)}, u32[]{:S(2)}, u32[]{:S(2)}) %collective-permute-start.2) | collective-permute-done | bytes 917536 | tf_op jit(solution)/shard_map/ppermute | solution.py:105
  184.5 4.5 convert_reduce_fusion.4
  194.8 15.2 %multiply_reduce_fusion.1 = (f32[8,448]{1,0:T(8,128)S(1)}, f32[8,448,1500]{2,1,0:T(8,128)}) fusion(f32[8,448,1500]{2,1,0:T(8,128)} %copy-done.1, f32[8,448]{1,0:T(8,128)S(1)} %log_add_fusion.2, bf16[448,8,64]{0,2,1:T(8,128)(2,1)} %bitcast.336, bf16[1500,8,64]{0,2,1:T(8,128)(2,1)} %bitcast.325), kind=kOutput, calls=%fused_computation.3 | convolution fusion | flops 709628416 | bytes 45031424 | tf_op jit(solution)/shard_map/lhe,khe->hlk/dot_general | solution.py:68
  209.9 15.0 %multiply_convert_fusion.1 = bf16[8,448,1500]{2,1,0:T(8,128)(2,1)S(1)} fusion(f32[8,448,1500]{2,1,0:T(8,128)} %get-tuple-element.167, f32[8,448,1500]{2,1,0:T(8,128)} %copy-done.1, f32[8,448]{1,0:T(8,128)S(1)} %get-tuple-element.166, f32[8,448]{1,0:T(8,128)S(1)} %log_add_fusion.2), kind=kLoop, calls=%fused_computation.2 | loop fusion | flops 26880000 | bytes 53788672 | tf_op jit(solution)/shard_map/convert_element_type | solution.py:70
  225.0 4.7 convert_reduce_fusion.9
  243.3 5.5 fusion.238
  265.1 9.0 multiply_reduce_fusion.5
  274.8 5.3 multiply_convert_fusion.3
  291.3 5.1 fusion.35
  299.1 5.3 collective-permute-done.3
  316.6 5.7 exponential_reduce_fusion
  324.4 10.5 fusion.138
  338.3 13.3 %convert_reduce_fusion.3 = (f32[8,64]{1,0:T(8,128)}, bf16[8,64,1500]{2,1,0:T(8,128)(2,1)}) fusion(bf16[448,8,64]{0,2,1:T(8,128)(2,1)} %bitcast.337, f32[8,448,1500]{2,1,0:T(8,128)} %copy-done.1, f32[8,448]{1,0:T(8,128)S(1)} %log_add_fusion.2), kind=kOutput, calls=%fused_computation.77 | convolution fusion | flops 706559488 | bytes 23515136 | tf_op jit(solution)/shard_map/hlk,lhe->khe/dot_general | solution.py:77
  374.8 15.9 %collective-permute-done.9 = bf16[448,1024]{1,0:T(8,128)(2,1)S(1)} collective-permute-done((bf16[448,1024]{1,0:T(8,128)(2,1)S(1)}, bf16[448,1024]{1,0:T(8,128)(2,1)S(1)}, u32[]{:S(2)}, u32[]{:S(2)}) %collective-permute-start.9) | collective-permute-done | bytes 917536 | tf_op jit(solution)/shard_map/ppermute | solution.py:105
  392.2 12.4 %collective-permute-done.5 = bf16[448,1024]{1,0:T(8,128)(2,1)S(1)} collective-permute-done((bf16[448,1024]{1,0:T(8,128)(2,1)S(1)}, bf16[448,1024]{1,0:T(8,128)(2,1)S(1)}, u32[]{:S(2)}, u32[]{:S(2)}) %collective-permute-start.5) | collective-permute-done | bytes 917536 | tf_op jit(solution)/shard_map/ppermute | solution.py:105
  413.4 11.7 convert_reduce_fusion.2
  426.4 5.4 fusion.113
  435.8 15.9 %multiply_reduce_fusion = (f32[8,448]{1,0:T(8,128)S(1)}, f32[8,448,1500]{2,1,0:T(8,128)}) fusion(f32[8,448,1500]{2,1,0:T(8,128)} %copy-done.2, f32[8,448]{1,0:T(8,128)S(1)} %log_add_fusion, bf16[448,8,64]{0,2,1:T(8,128)(2,1)} %bitcast.339, bf16[1500,8,64]{0,2,1:T(8,128)(2,1)} %bitcast.322), kind=kOutput, calls=%fused_computation.1 | convolution fusion | flops 709628416 | bytes 45031424 | tf_op jit(solution)/shard_map/lhe,khe->hlk/dot_general | solution.py:68
  451.8 15.0 %multiply_convert_fusion = bf16[8,448,1500]{2,1,0:T(8,128)(2,1)S(1)} fusion(f32[8,448,1500]{2,1,0:T(8,128)} %get-tuple-element.174, f32[8,448,1500]{2,1,0:T(8,128)} %copy-done.2, f32[8,448]{1,0:T(8,128)S(1)} %get-tuple-element.173, f32[8,448]{1,0:T(8,128)S(1)} %log_add_fusion), kind=kLoop, calls=%fused_computation | loop fusion | flops 26880000 | bytes 53788672 | tf_op jit(solution)/shard_map/convert_element_type | solution.py:70
  474.6 5.4 fusion.110
  480.6 8.0 convert_reduce_fusion.8
  492.1 5.8 convert_reduce_fusion.11
  500.7 7.0 collective-permute-done.10
  516.3 5.2 convert_reduce_fusion.10
  532.6 4.7 multiply_reduce_fusion.4
  555.2 8.9 convolution_convert_fusion.1
  576.1 28.9 %collective-permute-done.12 = bf16[1500,512]{1,0:T(8,128)(2,1)S(1)} collective-permute-done((bf16[1500,512]{1,0:T(8,128)(2,1)S(1)}, bf16[1500,512]{1,0:T(8,128)(2,1)S(1)}, u32[]{:S(2)}, u32[]{:S(2)}) %collective-permute-start.12) | collective-permute-done | bytes 1536032 | tf_op jit(solution)/shard_map/ppermute | solution.py:307
  607.7 6.2 convolution_convert_fusion
  627.8 4.6 pad_maximum_fusion.4
  636.5 21.2 %collective-permute-done.13 = bf16[1500,512]{1,0:T(8,128)(2,1)} collective-permute-done((bf16[1500,512]{1,0:T(8,128)(2,1)}, bf16[1500,512]{1,0:T(8,128)(2,1)}, u32[]{:S(2)}, u32[]{:S(2)}) %collective-permute-start.13) | collective-permute-done | bytes 1536032 | tf_op jit(solution)/shard_map/ppermute | solution.py:307
  662.3 12.7 %copy.122 = f32[2,1500,512]{2,0,1:T(2,128)} copy(f32[2,1500,512]{2,1,0:T(8,128)S(1)} %pad_maximum_fusion) | data formatting | bytes 12288000
  675.1 4.5 collective-permute-start.127
  707.2 62.8 %psum.7 = f32[13312]{0:T(1024)S(1)} all-reduce(f32[13312]{0:T(1024)} %add_dynamic-update-slice_fusion), channel_id=1, replica_groups=mesh['dp'=16,'tensor'=2] {'dp'}, use_global_device_ids=true, to_apply=%region_64.65 | all-reduce | flops 13312 | bytes 106496 | tf_op jit(solution)/shard_map/psum | solution.py:340
  770.6 5.7 collective-permute-done.109
  776.9 5.9 collective-permute-done.110
  789.5 4.5 collective-permute-start.82
  794.0 4.5 collective-permute-start.128
  855.4 4.5 collective-permute-start.102
  881.1 6.6 collective-permute-done.44
  888.5 6.3 collective-permute-done.45
  896.5 4.6 collective-permute-done.46
  902.9 4.8 collective-permute-done.47
  909.7 4.6 collective-permute-done.48
  920.7 4.5 collective-permute-start.67
  934.1 4.5 collective-permute-start.68
  969.9 4.5 collective-permute-start.54
  977.7 4.5 collective-permute-start.72
  1015.1 63.6 %reduce-scatter.29.cloned.1.call-done = bf16[128,1024]{1,0:T(8,128)(2,1)} async-done(((bf16[2048,1024]{1,0:T(8,128)(2,1)}), bf16[128,1024]{1,0:T(8,128)(2,1)}) %reduce-scatter.29.cloned.1.call-update) | async-done | bytes 262160 | tf_op jit(solution)/shard_map/reduce_scatter | solution.py:110
  1091.2 4.4 collective-permute-start.56
  1117.4 4.5 collective-permute-start.27
  1123.8 4.5 collective-permute-start.42
  1136.7 4.5 collective-permute-start.28
  1143.1 4.5 collective-permute-start.43
  1187.1 4.5 dynamic-slice_convert_fusion.1
  1192.4 4.4 dynamic-slice_convert_fusion
  (1065 shorter events, 559.3 us)
Async XLA Ops:
  7.2 620.6 %reduce-scatter.23.cloned.1.call-start = ((), (), s32[]{:S(2)}) async-start(), calls=%async_computation.16 | async-start | bytes 1114112 | tf_op jit(solution)/shard_map/reduce_scatter | solution.py:110
  38.2 35.6 %collective-permute-start = (bf16[448,1024]{1,0:T(8,128)(2,1)}, bf16[448,1024]{1,0:T(8,128)(2,1)}, u32[]{:S(2)}, u32[]{:S(2)}) collective-permute-start(bf16[448,1024]{1,0:T(8,128)(2,1)} %convolution_convert_fusion.14), channel_id=1, source_target_pairs={{0,1},{1,0},{2,3},{3,2},{4,5},{5,4},{6,7},{7,6},{8,9},{9,8},{10,11... | collective-permute-start | bytes 2752520 | tf_op jit(solution)/shard_map/ppermute | solution.py:105
  108.3 21.9 %collective-permute-start.1 = (bf16[448,1024]{1,0:T(8,128)(2,1)S(1)}, bf16[448,1024]{1,0:T(8,128)(2,1)S(1)}, u32[]{:S(2)}, u32[]{:S(2)}) collective-permute-start(bf16[448,1024]{1,0:T(8,128)(2,1)S(1)} %convolution_convert_fusion.13), channel_id=1, source_target_pairs={{0,1},{1,0},{2,3},{3,2},{4,5},{5,4},{6,7},{7,6},{8,9},{9,8},{10,11... | collective-permute-start | bytes 2752520 | tf_op jit(solution)/shard_map/ppermute | solution.py:105
  143.5 23.5 %collective-permute-start.6 = (bf16[448,1024]{1,0:T(8,128)(2,1)}, bf16[448,1024]{1,0:T(8,128)(2,1)}, u32[]{:S(2)}, u32[]{:S(2)}) collective-permute-start(bf16[448,1024]{1,0:T(8,128)(2,1)} %convolution_convert_fusion.16), channel_id=1, source_target_pairs={{0,1},{1,0},{2,3},{3,2},{4,5},{5,4},{6,7},{7,6},{8,9},{9,8},{10,11... | collective-permute-start | bytes 2752520 | tf_op jit(solution)/shard_map/ppermute | solution.py:105
  146.8 37.6 %collective-permute-start.2 = (bf16[448,1024]{1,0:T(8,128)(2,1)}, bf16[448,1024]{1,0:T(8,128)(2,1)}, u32[]{:S(2)}, u32[]{:S(2)}) collective-permute-start(bf16[448,1024]{1,0:T(8,128)(2,1)} %convolution_convert_fusion.18), channel_id=1, source_target_pairs={{0,1},{1,0},{2,3},{3,2},{4,5},{5,4},{6,7},{7,6},{8,9},{9,8},{10,11... | collective-permute-start | bytes 2752520 | tf_op jit(solution)/shard_map/ppermute | solution.py:105
  232.9 20.4 %collective-permute-start.7 = (bf16[448,1024]{1,0:T(8,128)(2,1)}, bf16[448,1024]{1,0:T(8,128)(2,1)}, u32[]{:S(2)}, u32[]{:S(2)}) collective-permute-start(bf16[448,1024]{1,0:T(8,128)(2,1)} %convolution_convert_fusion.10), channel_id=1, source_target_pairs={{0,1},{1,0},{2,3},{3,2},{4,5},{5,4},{6,7},{7,6},{8,9},{9,8},{10,11... | collective-permute-start | bytes 2752520 | tf_op jit(solution)/shard_map/ppermute | solution.py:105
  284.9 19.5 %collective-permute-start.3 = (bf16[448,1024]{1,0:T(8,128)(2,1)}, bf16[448,1024]{1,0:T(8,128)(2,1)}, u32[]{:S(2)}, u32[]{:S(2)}) collective-permute-start(bf16[448,1024]{1,0:T(8,128)(2,1)} %convolution_convert_fusion.12), channel_id=1, source_target_pairs={{0,1},{1,0},{2,3},{3,2},{4,5},{5,4},{6,7},{7,6},{8,9},{9,8},{10,11... | collective-permute-start | bytes 2752520 | tf_op jit(solution)/shard_map/ppermute | solution.py:105
  337.0 18.4 %collective-permute-start.4 = (bf16[448,1024]{1,0:T(8,128)(2,1)S(1)}, bf16[448,1024]{1,0:T(8,128)(2,1)S(1)}, u32[]{:S(2)}, u32[]{:S(2)}) collective-permute-start(bf16[448,1024]{1,0:T(8,128)(2,1)S(1)} %convolution_convert_fusion.11), channel_id=1, source_target_pairs={{0,1},{1,0},{2,3},{3,2},{4,5},{5,4},{6,7},{7,6},{8,9},{9,8},{10,11... | collective-permute-start | bytes 2752520 | tf_op jit(solution)/shard_map/ppermute | solution.py:105
  367.4 23.3 %collective-permute-start.9 = (bf16[448,1024]{1,0:T(8,128)(2,1)S(1)}, bf16[448,1024]{1,0:T(8,128)(2,1)S(1)}, u32[]{:S(2)}, u32[]{:S(2)}) collective-permute-start(bf16[448,1024]{1,0:T(8,128)(2,1)S(1)} %convolution_convert_fusion.15), channel_id=1, source_target_pairs={{0,1},{1,0},{2,3},{3,2},{4,5},{5,4},{6,7},{7,6},{8,9},{9,8},{10,11... | collective-permute-start | bytes 2752520 | tf_op jit(solution)/shard_map/ppermute | solution.py:105
  371.0 33.6 %collective-permute-start.5 = (bf16[448,1024]{1,0:T(8,128)(2,1)S(1)}, bf16[448,1024]{1,0:T(8,128)(2,1)S(1)}, u32[]{:S(2)}, u32[]{:S(2)}) collective-permute-start(bf16[448,1024]{1,0:T(8,128)(2,1)S(1)} %convolution_convert_fusion.17), channel_id=1, source_target_pairs={{0,1},{1,0},{2,3},{3,2},{4,5},{5,4},{6,7},{7,6},{8,9},{9,8},{10,11... | collective-permute-start | bytes 2752520 | tf_op jit(solution)/shard_map/ppermute | solution.py:105
  431.8 243.3 %reduce-scatter.25.cloned.1.call-start = ((), (), s32[]{:S(2)}) async-start(), calls=%async_computation.17 | async-start | bytes 1114112 | tf_op jit(solution)/shard_map/reduce_scatter | solution.py:110
  451.7 232.6 %reduce-scatter.21.cloned.1.call-start = ((), (), s32[]{:S(2)}) async-start(), calls=%async_computation.15 | async-start | bytes 1114112 | tf_op jit(solution)/shard_map/reduce_scatter | solution.py:110
  480.1 309.4 %reduce-scatter.19.cloned.1.call-start = ((), (), s32[]{:S(2)}) async-start(), calls=%async_computation.14 | async-start | bytes 1114112 | tf_op jit(solution)/shard_map/reduce_scatter | solution.py:110
  490.4 17.3 %collective-permute-start.10 = (bf16[448,1024]{1,0:T(8,128)(2,1)}, bf16[448,1024]{1,0:T(8,128)(2,1)}, u32[]{:S(2)}, u32[]{:S(2)}) collective-permute-start(bf16[448,1024]{1,0:T(8,128)(2,1)} %convolution_convert_fusion.9), channel_id=1, source_target_pairs={{0,1},{1,0},{2,3},{3,2},{4,5},{5,4},{6,7},{7,6},{8,9},{9,8},{10,11... | collective-permute-start | bytes 2752520 | tf_op jit(solution)/shard_map/ppermute | solution.py:105
  500.5 380.5 %reduce-scatter.15.cloned.1.call-start = ((), (), s32[]{:S(2)}) async-start(), calls=%async_computation.12 | async-start | bytes 1114112 | tf_op jit(solution)/shard_map/reduce_scatter | solution.py:110
  524.9 356.2 %reduce-scatter.17.cloned.1.call-start = ((), (), s32[]{:S(2)}) async-start(), calls=%async_computation.13 | async-start | bytes 1114112 | tf_op jit(solution)/shard_map/reduce_scatter | solution.py:110
  532.1 401.8 %reduce-scatter.11.cloned.1.call-start = ((), (), s32[]{:S(2)}) async-start(), calls=%async_computation.10 | async-start | bytes 1114112 | tf_op jit(solution)/shard_map/reduce_scatter | solution.py:110
  547.5 386.4 %reduce-scatter.13.cloned.1.call-start = ((), (), s32[]{:S(2)}) async-start(), calls=%async_computation.11 | async-start | bytes 1114112 | tf_op jit(solution)/shard_map/reduce_scatter | solution.py:110
  555.1 457.9 %reduce-scatter.27.cloned.1.call-start = ((), (), s32[]{:S(2)}) async-start(), calls=%async_computation.18 | async-start | bytes 4456448 | tf_op jit(solution)/shard_map/reduce_scatter | solution.py:110
  564.1 514.6 %reduce-scatter.29.cloned.1.call-start = ((), (), s32[]{:S(2)}) async-start(), calls=%async_computation.19 | async-start | bytes 4456448 | tf_op jit(solution)/shard_map/reduce_scatter | solution.py:110
  568.3 36.6 %collective-permute-start.12 = (bf16[1500,512]{1,0:T(8,128)(2,1)S(1)}, bf16[1500,512]{1,0:T(8,128)(2,1)S(1)}, u32[]{:S(2)}, u32[]{:S(2)}) collective-permute-start(bf16[1500,512]{1,0:T(8,128)(2,1)S(1)} %fusion.36), channel_id=1, source_target_pairs={{0,1},{1,0},{2,3},{3,2},{4,5},{5,4},{6,7},{7,6},{8,9},{9,8},{10,11... | collective-permute-start | bytes 4608008 | tf_op jit(solution)/shard_map/ppermute | solution.py:307
  575.6 104.3 %collective-permute-start.8 = (bf16[448,1024]{1,0:T(8,128)(2,1)}, bf16[448,1024]{1,0:T(8,128)(2,1)}, u32[]{:S(2)}, u32[]{:S(2)}) collective-permute-start(bf16[448,1024]{1,0:T(8,128)(2,1)} %add_convert_fusion.1), channel_id=1, source_target_pairs={{0,1},{1,0},{2,3},{3,2},{4,5},{5,4},{6,7},{7,6},{8,9},{9,8},{10,11... | collective-permute-start | bytes 2752520 | tf_op jit(solution)/shard_map/ppermute | solution.py:105
  619.1 38.6 %collective-permute-start.13 = (bf16[1500,512]{1,0:T(8,128)(2,1)}, bf16[1500,512]{1,0:T(8,128)(2,1)}, u32[]{:S(2)}, u32[]{:S(2)}) collective-permute-start(bf16[1500,512]{1,0:T(8,128)(2,1)} %fusion.37), channel_id=1, source_target_pairs={{0,1},{1,0},{2,3},{3,2},{4,5},{5,4},{6,7},{7,6},{8,9},{9,8},{10,11... | collective-permute-start | bytes 4608008 | tf_op jit(solution)/shard_map/ppermute | solution.py:307
  627.5 57.0 %collective-permute-start.11 = (bf16[448,1024]{1,0:T(8,128)(2,1)}, bf16[448,1024]{1,0:T(8,128)(2,1)}, u32[]{:S(2)}, u32[]{:S(2)}) collective-permute-start(bf16[448,1024]{1,0:T(8,128)(2,1)} %add_convert_fusion), channel_id=1, source_target_pairs={{0,1},{1,0},{2,3},{3,2},{4,5},{5,4},{6,7},{7,6},{8,9},{9,8},{10,11... | collective-permute-start | bytes 2752520 | tf_op jit(solution)/shard_map/ppermute | solution.py:105
  635.0 26.3 %collective-permute-start.105 = (bf16[64,512]{1,0:T(8,128)(2,1)S(1)}, bf16[64,512]{1,0:T(8,128)(2,1)S(1)}, u32[]{:S(2)}, u32[]{:S(2)}) collective-permute-start(bf16[64,512]{1,0:T(8,128)(2,1)S(1)} %collective-permute-done.104), channel_id=1, source_target_pairs={{0,2},{2,4},{4,6},{6,8},{8,10},{10,12},{12,14},{14,16},{16,18},{18... | collective-permute-start | bytes 196616 | tf_op jit(solution)/shard_map/ppermute | solution.py:19
  661.3 23.1 %collective-permute-start.106 = (bf16[64,512]{1,0:T(8,128)(2,1)S(1)}, bf16[64,512]{1,0:T(8,128)(2,1)S(1)}, u32[]{:S(2)}, u32[]{:S(2)}) collective-permute-start(bf16[64,512]{1,0:T(8,128)(2,1)S(1)} %collective-permute-done.105), channel_id=1, source_target_pairs={{0,2},{2,4},{4,6},{6,8},{8,10},{10,12},{12,14},{14,16},{16,18},{18... | collective-permute-start | bytes 196616 | tf_op jit(solution)/shard_map/ppermute | solution.py:19
  675.1 114.4 %collective-permute-start.127 = (bf16[32,1024]{1,0:T(8,128)(2,1)}, bf16[32,1024]{1,0:T(8,128)(2,1)S(1)}, u32[]{:S(2)}, u32[]{:S(2)}) collective-permute-start(bf16[32,1024]{1,0:T(8,128)(2,1)} %reduce-scatter.25.cloned.1.call-done), channel_id=1, source_target_pairs={{0,30},{2,0},{4,2},{6,4},{8,6},{10,8},{12,10},{14,12},{16,14},{18,... | collective-permute-start | bytes 196616 | tf_op jit(solution)/shard_map/ppermute | solution.py:21
  679.5 114.5 %collective-permute-start.119 = (bf16[32,1024]{1,0:T(8,128)(2,1)}, bf16[32,1024]{1,0:T(8,128)(2,1)S(1)}, u32[]{:S(2)}, u32[]{:S(2)}) collective-permute-start(bf16[32,1024]{1,0:T(8,128)(2,1)} %reduce-scatter.25.cloned.1.call-done), channel_id=1, source_target_pairs={{0,2},{2,4},{4,6},{6,8},{8,10},{10,12},{12,14},{14,16},{16,18},{18... | collective-permute-start | bytes 196616 | tf_op jit(solution)/shard_map/ppermute | solution.py:19
  680.0 114.0 %collective-permute-start.112 = (bf16[64,512]{1,0:T(8,128)(2,1)S(1)}, bf16[64,512]{1,0:T(8,128)(2,1)S(1)}, u32[]{:S(2)}, u32[]{:S(2)}) collective-permute-start(bf16[64,512]{1,0:T(8,128)(2,1)S(1)} %copy-done.110), channel_id=1, source_target_pairs={{0,30},{2,0},{4,2},{6,4},{8,6},{10,8},{12,10},{14,12},{16,14},{18,... | collective-permute-start | bytes 196616 | tf_op jit(solution)/shard_map/ppermute | solution.py:21
  684.4 114.1 %collective-permute-start.97 = (bf16[64,512]{1,0:T(8,128)(2,1)}, bf16[64,512]{1,0:T(8,128)(2,1)S(1)}, u32[]{:S(2)}, u32[]{:S(2)}) collective-permute-start(bf16[64,512]{1,0:T(8,128)(2,1)} %reduce-scatter.21.cloned.1.call-done), channel_id=1, source_target_pairs={{0,30},{2,0},{4,2},{6,4},{8,6},{10,8},{12,10},{14,12},{16,14},{18,... | collective-permute-start | bytes 196616 | tf_op jit(solution)/shard_map/ppermute | solution.py:21
  684.5 17.6 %collective-permute-start.107 = (bf16[64,512]{1,0:T(8,128)(2,1)S(1)}, bf16[64,512]{1,0:T(8,128)(2,1)S(1)}, u32[]{:S(2)}, u32[]{:S(2)}) collective-permute-start(bf16[64,512]{1,0:T(8,128)(2,1)S(1)} %collective-permute-done.106), channel_id=1, source_target_pairs={{0,2},{2,4},{4,6},{6,8},{8,10},{10,12},{12,14},{14,16},{16,18},{18... | collective-permute-start | bytes 196616 | tf_op jit(solution)/shard_map/ppermute | solution.py:19
  702.1 67.8 %collective-permute-start.108 = (bf16[64,512]{1,0:T(8,128)(2,1)S(1)}, bf16[64,512]{1,0:T(8,128)(2,1)S(1)}, u32[]{:S(2)}, u32[]{:S(2)}) collective-permute-start(bf16[64,512]{1,0:T(8,128)(2,1)S(1)} %collective-permute-done.107), channel_id=1, source_target_pairs={{0,2},{2,4},{4,6},{6,8},{8,10},{10,12},{12,14},{14,16},{16,18},{18... | collective-permute-start | bytes 196616 | tf_op jit(solution)/shard_map/ppermute | solution.py:19
  789.5 13.4 %collective-permute-start.82 = (bf16[64,512]{1,0:T(8,128)(2,1)}, bf16[64,512]{1,0:T(8,128)(2,1)S(1)}, u32[]{:S(2)}, u32[]{:S(2)}) collective-permute-start(bf16[64,512]{1,0:T(8,128)(2,1)} %reduce-scatter.19.cloned.1.call-done), channel_id=1, source_target_pairs={{0,30},{2,0},{4,2},{6,4},{8,6},{10,8},{12,10},{14,12},{16,14},{18,... | collective-permute-start | bytes 196616 | tf_op jit(solution)/shard_map/ppermute | solution.py:21
  803.5 13.0 %collective-permute-start.83 = (bf16[64,512]{1,0:T(8,128)(2,1)S(1)}, bf16[64,512]{1,0:T(8,128)(2,1)S(1)}, u32[]{:S(2)}, u32[]{:S(2)}) collective-permute-start(bf16[64,512]{1,0:T(8,128)(2,1)S(1)} %collective-permute-done.82), channel_id=1, source_target_pairs={{0,30},{2,0},{4,2},{6,4},{8,6},{10,8},{12,10},{14,12},{16,14},{18,... | collective-permute-start | bytes 196616 | tf_op jit(solution)/shard_map/ppermute | solution.py:21
  835.1 13.0 %collective-permute-start.131 = (bf16[32,1024]{1,0:T(8,128)(2,1)S(1)}, bf16[32,1024]{1,0:T(8,128)(2,1)S(1)}, u32[]{:S(2)}, u32[]{:S(2)}) collective-permute-start(bf16[32,1024]{1,0:T(8,128)(2,1)S(1)} %collective-permute-done.130), channel_id=1, source_target_pairs={{0,30},{2,0},{4,2},{6,4},{8,6},{10,8},{12,10},{14,12},{16,14},{18,... | collective-permute-start | bytes 196616 | tf_op jit(solution)/shard_map/ppermute | solution.py:21
  865.3 55.4 %collective-permute-start.133 = (bf16[32,1024]{1,0:T(8,128)(2,1)S(1)}, bf16[32,1024]{1,0:T(8,128)(2,1)S(1)}, u32[]{:S(2)}, u32[]{:S(2)}) collective-permute-start(bf16[32,1024]{1,0:T(8,128)(2,1)S(1)} %collective-permute-done.132), channel_id=1, source_target_pairs={{0,30},{2,0},{4,2},{6,4},{8,6},{10,8},{12,10},{14,12},{16,14},{18,... | collective-permute-start | bytes 196616 | tf_op jit(solution)/shard_map/ppermute | solution.py:21
  920.7 13.3 %collective-permute-start.67 = (bf16[32,1024]{1,0:T(8,128)(2,1)}, bf16[32,1024]{1,0:T(8,128)(2,1)S(1)}, u32[]{:S(2)}, u32[]{:S(2)}) collective-permute-start(bf16[32,1024]{1,0:T(8,128)(2,1)} %reduce-scatter.17.cloned.1.call-done), channel_id=1, source_target_pairs={{0,30},{2,0},{4,2},{6,4},{8,6},{10,8},{12,10},{14,12},{16,14},{18,... | collective-permute-start | bytes 196616 | tf_op jit(solution)/shard_map/ppermute | solution.py:21
  929.5 24.9 %collective-permute-start.52 = (bf16[64,512]{1,0:T(8,128)(2,1)S(1)}, bf16[64,512]{1,0:T(8,128)(2,1)}, u32[]{:S(2)}, u32[]{:S(2)}) collective-permute-start(bf16[64,512]{1,0:T(8,128)(2,1)S(1)} %copy-done.105), channel_id=1, source_target_pairs={{0,30},{2,0},{4,2},{6,4},{8,6},{10,8},{12,10},{14,12},{16,14},{18,... | collective-permute-start | bytes 196616 | tf_op jit(solution)/shard_map/ppermute | solution.py:21
  940.5 19.2 %collective-permute-start.22 = (bf16[64,512]{1,0:T(8,128)(2,1)}, bf16[64,512]{1,0:T(8,128)(2,1)S(1)}, u32[]{:S(2)}, u32[]{:S(2)}) collective-permute-start(bf16[64,512]{1,0:T(8,128)(2,1)} %reduce-scatter.11.cloned.1.call-done), channel_id=1, source_target_pairs={{0,30},{2,0},{4,2},{6,4},{8,6},{10,8},{12,10},{14,12},{16,14},{18,... | collective-permute-start | bytes 196616 | tf_op jit(solution)/shard_map/ppermute | solution.py:21
  961.7 12.6 %collective-permute-start.38 = (bf16[64,512]{1,0:T(8,128)(2,1)S(1)}, bf16[64,512]{1,0:T(8,128)(2,1)S(1)}, u32[]{:S(2)}, u32[]{:S(2)}) collective-permute-start(bf16[64,512]{1,0:T(8,128)(2,1)S(1)} %collective-permute-done.37), channel_id=1, source_target_pairs={{0,30},{2,0},{4,2},{6,4},{8,6},{10,8},{12,10},{14,12},{16,14},{18,... | collective-permute-start | bytes 196616 | tf_op jit(solution)/shard_map/ppermute | solution.py:21
  962.1 12.4 %collective-permute-start.17 = (bf16[64,512]{1,0:T(8,128)(2,1)S(1)}, bf16[64,512]{1,0:T(8,128)(2,1)S(1)}, u32[]{:S(2)}, u32[]{:S(2)}) collective-permute-start(bf16[64,512]{1,0:T(8,128)(2,1)S(1)} %collective-permute-done.16), channel_id=1, source_target_pairs={{0,2},{2,4},{4,6},{6,8},{8,10},{10,12},{12,14},{14,16},{16,18},{18... | collective-permute-start | bytes 196616 | tf_op jit(solution)/shard_map/ppermute | solution.py:19
  974.4 14.9 %collective-permute-start.39 = (bf16[64,512]{1,0:T(8,128)(2,1)S(1)}, bf16[64,512]{1,0:T(8,128)(2,1)}, u32[]{:S(2)}, u32[]{:S(2)}) collective-permute-start(bf16[64,512]{1,0:T(8,128)(2,1)S(1)} %collective-permute-done.38), channel_id=1, source_target_pairs={{0,30},{2,0},{4,2},{6,4},{8,6},{10,8},{12,10},{14,12},{16,14},{18,... | collective-permute-start | bytes 196616 | tf_op jit(solution)/shard_map/ppermute | solution.py:21
  984.9 98.5 %collective-permute-start.55 = (bf16[64,512]{1,0:T(8,128)(2,1)}, bf16[64,512]{1,0:T(8,128)(2,1)}, u32[]{:S(2)}, u32[]{:S(2)}) collective-permute-start(bf16[64,512]{1,0:T(8,128)(2,1)} %collective-permute-done.54), channel_id=1, source_target_pairs={{0,30},{2,0},{4,2},{6,4},{8,6},{10,8},{12,10},{14,12},{16,14},{18,... | collective-permute-start | bytes 196616 | tf_op jit(solution)/shard_map/ppermute | solution.py:21
  989.3 98.0 %collective-permute-start.25 = (bf16[64,512]{1,0:T(8,128)(2,1)}, bf16[64,512]{1,0:T(8,128)(2,1)}, u32[]{:S(2)}, u32[]{:S(2)}) collective-permute-start(bf16[64,512]{1,0:T(8,128)(2,1)} %collective-permute-done.24), channel_id=1, source_target_pairs={{0,30},{2,0},{4,2},{6,4},{8,6},{10,8},{12,10},{14,12},{16,14},{18,... | collective-permute-start | bytes 196616 | tf_op jit(solution)/shard_map/ppermute | solution.py:21
  989.4 101.8 %collective-permute-start.40 = (bf16[64,512]{1,0:T(8,128)(2,1)}, bf16[64,512]{1,0:T(8,128)(2,1)}, u32[]{:S(2)}, u32[]{:S(2)}) collective-permute-start(bf16[64,512]{1,0:T(8,128)(2,1)} %collective-permute-done.39), channel_id=1, source_target_pairs={{0,30},{2,0},{4,2},{6,4},{8,6},{10,8},{12,10},{14,12},{16,14},{18,... | collective-permute-start | bytes 196616 | tf_op jit(solution)/shard_map/ppermute | solution.py:21
  996.9 17.4 %collective-permute-start.73 = (bf16[32,1024]{1,0:T(8,128)(2,1)}, bf16[32,1024]{1,0:T(8,128)(2,1)}, u32[]{:S(2)}, u32[]{:S(2)}) collective-permute-start(bf16[32,1024]{1,0:T(8,128)(2,1)} %collective-permute-done.72), channel_id=1, source_target_pairs={{0,30},{2,0},{4,2},{6,4},{8,6},{10,8},{12,10},{14,12},{16,14},{18,... | collective-permute-start | bytes 196616 | tf_op jit(solution)/shard_map/ppermute | solution.py:21
  1013.0 65.7 %collective-permute-start.134 = (bf16[64,2048]{1,0:T(8,128)(2,1)}, bf16[64,2048]{1,0:T(8,128)(2,1)}, u32[]{:S(2)}, u32[]{:S(2)}) collective-permute-start(bf16[64,2048]{1,0:T(8,128)(2,1)} %reduce-scatter.27.cloned.1.call-done), channel_id=1, source_target_pairs={{0,2},{2,4},{4,6},{6,8},{8,10},{10,12},{12,14},{14,16},{16,18},{18... | collective-permute-start | bytes 786440 | tf_op jit(solution)/shard_map/ppermute | solution.py:19
  1083.4 25.4 %collective-permute-start.142 = (bf16[64,2048]{1,0:T(8,128)(2,1)S(1)}, bf16[64,2048]{1,0:T(8,128)(2,1)S(1)}, u32[]{:S(2)}, u32[]{:S(2)}) collective-permute-start(bf16[64,2048]{1,0:T(8,128)(2,1)S(1)} %copy-done.73), channel_id=1, source_target_pairs={{0,30},{2,0},{4,2},{6,4},{8,6},{10,8},{12,10},{14,12},{16,14},{18,... | collective-permute-start | bytes 786440 | tf_op jit(solution)/shard_map/ppermute | solution.py:21
  1087.4 21.5 %collective-permute-start.157 = (bf16[128,1024]{1,0:T(8,128)(2,1)S(1)}, bf16[128,1024]{1,0:T(8,128)(2,1)S(1)}, u32[]{:S(2)}, u32[]{:S(2)}) collective-permute-start(bf16[128,1024]{1,0:T(8,128)(2,1)S(1)} %copy-done.74), channel_id=1, source_target_pairs={{0,30},{2,0},{4,2},{6,4},{8,6},{10,8},{12,10},{14,12},{16,14},{18,... | collective-permute-start | bytes 786440 | tf_op jit(solution)/shard_map/ppermute | solution.py:21
  1087.8 21.1 %collective-permute-start.150 = (bf16[128,1024]{1,0:T(8,128)(2,1)S(1)}, bf16[128,1024]{1,0:T(8,128)(2,1)S(1)}, u32[]{:S(2)}, u32[]{:S(2)}) collective-permute-start(bf16[128,1024]{1,0:T(8,128)(2,1)S(1)} %collective-permute-done.149), channel_id=1, source_target_pairs={{0,2},{2,4},{4,6},{6,8},{8,10},{10,12},{12,14},{14,16},{16,18},{18... | collective-permute-start | bytes 786440 | tf_op jit(solution)/shard_map/ppermute | solution.py:19
  1090.3 19.1 %collective-permute-start.136 = (bf16[64,2048]{1,0:T(8,128)(2,1)S(1)}, bf16[64,2048]{1,0:T(8,128)(2,1)S(1)}, u32[]{:S(2)}, u32[]{:S(2)}) collective-permute-start(bf16[64,2048]{1,0:T(8,128)(2,1)S(1)} %collective-permute-done.135), channel_id=1, source_target_pairs={{0,2},{2,4},{4,6},{6,8},{8,10},{10,12},{12,14},{14,16},{16,18},{18... | collective-permute-start | bytes 786440 | tf_op jit(solution)/shard_map/ppermute | solution.py:19
  1108.8 19.5 %collective-permute-start.143 = (bf16[64,2048]{1,0:T(8,128)(2,1)S(1)}, bf16[64,2048]{1,0:T(8,128)(2,1)S(1)}, u32[]{:S(2)}, u32[]{:S(2)}) collective-permute-start(bf16[64,2048]{1,0:T(8,128)(2,1)S(1)} %collective-permute-done.142), channel_id=1, source_target_pairs={{0,30},{2,0},{4,2},{6,4},{8,6},{10,8},{12,10},{14,12},{16,14},{18,... | collective-permute-start | bytes 786440 | tf_op jit(solution)/shard_map/ppermute | solution.py:21
  1108.9 19.5 %collective-permute-start.158 = (bf16[128,1024]{1,0:T(8,128)(2,1)S(1)}, bf16[128,1024]{1,0:T(8,128)(2,1)S(1)}, u32[]{:S(2)}, u32[]{:S(2)}) collective-permute-start(bf16[128,1024]{1,0:T(8,128)(2,1)S(1)} %collective-permute-done.157), channel_id=1, source_target_pairs={{0,30},{2,0},{4,2},{6,4},{8,6},{10,8},{12,10},{14,12},{16,14},{18,... | collective-permute-start | bytes 786440 | tf_op jit(solution)/shard_map/ppermute | solution.py:21
  1108.9 19.5 %collective-permute-start.151 = (bf16[128,1024]{1,0:T(8,128)(2,1)S(1)}, bf16[128,1024]{1,0:T(8,128)(2,1)S(1)}, u32[]{:S(2)}, u32[]{:S(2)}) collective-permute-start(bf16[128,1024]{1,0:T(8,128)(2,1)S(1)} %collective-permute-done.150), channel_id=1, source_target_pairs={{0,2},{2,4},{4,6},{6,8},{8,10},{10,12},{12,14},{14,16},{16,18},{18... | collective-permute-start | bytes 786440 | tf_op jit(solution)/shard_map/ppermute | solution.py:19
  1109.4 19.5 %collective-permute-start.137 = (bf16[64,2048]{1,0:T(8,128)(2,1)S(1)}, bf16[64,2048]{1,0:T(8,128)(2,1)S(1)}, u32[]{:S(2)}, u32[]{:S(2)}) collective-permute-start(bf16[64,2048]{1,0:T(8,128)(2,1)S(1)} %collective-permute-done.136), channel_id=1, source_target_pairs={{0,2},{2,4},{4,6},{6,8},{8,10},{10,12},{12,14},{14,16},{16,18},{18... | collective-permute-start | bytes 786440 | tf_op jit(solution)/shard_map/ppermute | solution.py:19
  1128.3 19.3 %collective-permute-start.144 = (bf16[64,2048]{1,0:T(8,128)(2,1)S(1)}, bf16[64,2048]{1,0:T(8,128)(2,1)S(1)}, u32[]{:S(2)}, u32[]{:S(2)}) collective-permute-start(bf16[64,2048]{1,0:T(8,128)(2,1)S(1)} %collective-permute-done.143), channel_id=1, source_target_pairs={{0,30},{2,0},{4,2},{6,4},{8,6},{10,8},{12,10},{14,12},{16,14},{18,... | collective-permute-start | bytes 786440 | tf_op jit(solution)/shard_map/ppermute | solution.py:21
  1128.4 19.3 %collective-permute-start.159 = (bf16[128,1024]{1,0:T(8,128)(2,1)S(1)}, bf16[128,1024]{1,0:T(8,128)(2,1)S(1)}, u32[]{:S(2)}, u32[]{:S(2)}) collective-permute-start(bf16[128,1024]{1,0:T(8,128)(2,1)S(1)} %collective-permute-done.158), channel_id=1, source_target_pairs={{0,30},{2,0},{4,2},{6,4},{8,6},{10,8},{12,10},{14,12},{16,14},{18,... | collective-permute-start | bytes 786440 | tf_op jit(solution)/shard_map/ppermute | solution.py:21
  1128.4 19.3 %collective-permute-start.152 = (bf16[128,1024]{1,0:T(8,128)(2,1)S(1)}, bf16[128,1024]{1,0:T(8,128)(2,1)S(1)}, u32[]{:S(2)}, u32[]{:S(2)}) collective-permute-start(bf16[128,1024]{1,0:T(8,128)(2,1)S(1)} %collective-permute-done.151), channel_id=1, source_target_pairs={{0,2},{2,4},{4,6},{6,8},{8,10},{10,12},{12,14},{14,16},{16,18},{18... | collective-permute-start | bytes 786440 | tf_op jit(solution)/shard_map/ppermute | solution.py:19
  1128.9 19.3 %collective-permute-start.138 = (bf16[64,2048]{1,0:T(8,128)(2,1)S(1)}, bf16[64,2048]{1,0:T(8,128)(2,1)S(1)}, u32[]{:S(2)}, u32[]{:S(2)}) collective-permute-start(bf16[64,2048]{1,0:T(8,128)(2,1)S(1)} %collective-permute-done.137), channel_id=1, source_target_pairs={{0,2},{2,4},{4,6},{6,8},{8,10},{10,12},{12,14},{14,16},{16,18},{18... | collective-permute-start | bytes 786440 | tf_op jit(solution)/shard_map/ppermute | solution.py:19
  1143.1 29.8 %collective-permute-start.43 = (bf16[64,512]{1,0:T(8,128)(2,1)S(1)}, bf16[64,512]{1,0:T(8,128)(2,1)S(1)}, u32[]{:S(2)}, u32[]{:S(2)}) collective-permute-start(bf16[64,512]{1,0:T(8,128)(2,1)S(1)} %collective-permute-done.42), channel_id=1, source_target_pairs={{0,30},{2,0},{4,2},{6,4},{8,6},{10,8},{12,10},{14,12},{16,14},{18,... | collective-permute-start | bytes 196616 | tf_op jit(solution)/shard_map/ppermute | solution.py:21
  1148.2 12.7 %collective-permute-start.139 = (bf16[64,2048]{1,0:T(8,128)(2,1)S(1)}, bf16[64,2048]{1,0:T(8,128)(2,1)S(1)}, u32[]{:S(2)}, u32[]{:S(2)}) collective-permute-start(bf16[64,2048]{1,0:T(8,128)(2,1)S(1)} %collective-permute-done.138), channel_id=1, source_target_pairs={{0,2},{2,4},{4,6},{6,8},{8,10},{10,12},{12,14},{14,16},{16,18},{18... | collective-permute-start | bytes 786440 | tf_op jit(solution)/shard_map/ppermute | solution.py:19
  1153.3 14.3 %collective-permute-start.146 = (bf16[64,2048]{1,0:T(8,128)(2,1)S(1)}, bf16[64,2048]{1,0:T(8,128)(2,1)S(1)}, u32[]{:S(2)}, u32[]{:S(2)}) collective-permute-start(bf16[64,2048]{1,0:T(8,128)(2,1)S(1)} %collective-permute-done.145), channel_id=1, source_target_pairs={{0,30},{2,0},{4,2},{6,4},{8,6},{10,8},{12,10},{14,12},{16,14},{18,... | collective-permute-start | bytes 786440 | tf_op jit(solution)/shard_map/ppermute | solution.py:21
  1171.1 13.2 %collective-permute-start.141 = (bf16[64,2048]{1,0:T(8,128)(2,1)S(1)}, bf16[64,2048]{1,0:T(8,128)(2,1)S(1)}, u32[]{:S(2)}, u32[]{:S(2)}) collective-permute-start(bf16[64,2048]{1,0:T(8,128)(2,1)S(1)} %collective-permute-done.140), channel_id=1, source_target_pairs={{0,2},{2,4},{4,6},{6,8},{8,10},{10,12},{12,14},{14,16},{16,18},{18... | collective-permute-start | bytes 786440 | tf_op jit(solution)/shard_map/ppermute | solution.py:19
  1179.5 12.5 %collective-permute-start.163 = (bf16[128,1024]{1,0:T(8,128)(2,1)S(1)}, bf16[128,1024]{1,0:T(8,128)(2,1)S(1)}, u32[]{:S(2)}, u32[]{:S(2)}) collective-permute-start(bf16[128,1024]{1,0:T(8,128)(2,1)S(1)} %collective-permute-done.162), channel_id=1, source_target_pairs={{0,30},{2,0},{4,2},{6,4},{8,6},{10,8},{12,10},{14,12},{16,14},{18,... | collective-permute-start | bytes 786440 | tf_op jit(solution)/shard_map/ppermute | solution.py:21
  (290 other events, 2806.6 us)
Sparse Core Ops, SparseCore 0:
  431.9 58.0 reduce-scatter.22
  493.6 56.6 reduce-scatter.24
  554.0 56.6 reduce-scatter.20
  614.1 56.5 reduce-scatter.18
  674.2 56.8 reduce-scatter.14
  734.5 57.2 reduce-scatter.16
  795.5 58.2 reduce-scatter.10
  857.4 58.4 reduce-scatter.12
  920.4 81.6 reduce-scatter.26
  1006.3 72.3 reduce-scatter.28
